TPU v7x, 128 devices: a whole 4x4x4 slice. The times are simulated.
128 devices in a mesh: row: 8 (over x, core), col: 16 (over z, y).
Axes of the slice: x: 4, y: 4, z: 4, core: 2. Of those that a mesh axis runs over, the one named last changes fastest.
Arguments:
- observed: bfloat16 [4096, 8, 128, 128], P(('row', 'col')), may hold values from -6 to 6
- sku_ids: int32 [4096], P(('row', 'col')), may hold values from 0 to 15
- store_ids: int32 [4096, 8], P(('row', 'col')), may hold values from 0 to 79
- live_slot_counts: int32 [8, 16, 8], P('row', 'col'), may hold values from 0 to 4, as said below
- sku_factors: float32 [262144, 256], P(('row', 'col')), may hold values from -1.5 to 1.5
- store_factors: float32 [81920, 256], P(('row', 'col')), may hold values from -1.5 to 1.5
Outputs:
- new_sku_factors: float32 [262144, 256], P(('row', 'col'))
- new_store_factors: float32 [81920, 256], P(('row', 'col'))
Inputs may be any that keep to these rules, and one draw needn't show every extreme that they name: `live_slot_counts`: in every column index some owner row's slots are full from every device of that column.
All inputs are finite; a program needn't handle non-finite values.
Results may differ from a plain program's by a relative error of at most 0.023.
Values may be sent and summed in bfloat16 or wider, within the bound.
A program may use at most 192 MiB of HBM per device.

v0:
```python
import jax
import jax.numpy as jnp
from jax import lax
from jax.sharding import PartitionSpec as P

learn_rate = 0.01
weight_decay = 0.05
group_rows = 8


def one_hot_of(ids, count):
    return (
        ids[..., None] == lax.broadcasted_iota(jnp.int32, ids.shape + (count,), ids.ndim)
    ).astype(jnp.bfloat16)


def pick_blocks(table, ids):
    selector = one_hot_of(ids.reshape(-1), table.shape[0])
    flat_table = table.reshape(table.shape[0], -1)
    picked = jnp.dot(selector, flat_table, preferred_element_type=jnp.float32).astype(jnp.bfloat16)
    return picked.reshape(ids.shape + table.shape[1:])


def sum_into_blocks(selector, values):
    flat_values = values.reshape(values.shape[0], -1)
    high_part = flat_values.astype(jnp.bfloat16)
    low_part = (flat_values - high_part.astype(jnp.float32)).astype(jnp.bfloat16)
    upper = jnp.einsum("nv,nx->vx", selector, high_part, preferred_element_type=jnp.float32)
    lower = jnp.einsum("nv,nx->vx", selector, low_part, preferred_element_type=jnp.float32)
    return upper + lower


def local(observed, sku_ids, store_ids, live_slot_counts, sku_factors, store_factors):
    rows_per_owner = lax.axis_size("row")
    total_live_slots = observed.shape[0]
    owner_wise = total_live_slots // rows_per_owner
    block_len = observed.shape[2]
    rank_len = sku_factors.shape[1]
    slot_alive_mask = lax.broadcasted_iota(
        jnp.int32, (rows_per_owner, owner_wise), 1
    ) < live_slot_counts.reshape(rows_per_owner, 1)
    slot_alive_mask = slot_alive_mask.reshape(total_live_slots).astype(jnp.float32)
    own_sku = sku_factors.reshape(-1, block_len, rank_len)
    own_table = own_sku.astype(jnp.bfloat16)
    own_store = store_factors.reshape(-1, block_len, rank_len)
    requested_ids = sku_ids.reshape(rows_per_owner, owner_wise)
    all_tables = lax.all_gather(own_table, "row", axis=0, tiled=True)
    owner_row = jnp.arange(total_live_slots, dtype=jnp.int32) // owner_wise
    fetched = pick_blocks(all_tables, owner_row * own_table.shape[0] + sku_ids)
    group_low = lax.all_gather(own_store.astype(jnp.bfloat16), "col", axis=0, tiled=True)
    group_count = group_low.shape[0]
    count_groups = total_live_slots // group_rows

    def split_into_groups(array_in):
        return array_in.reshape((count_groups, group_rows) + array_in.shape[1:])

    input_arrays = (
        split_into_groups(fetched),
        split_into_groups(observed),
        split_into_groups(store_ids),
        split_into_groups(slot_alive_mask),
    )

    def misfit_of(factor_rows, measured, store_pick, store_table):
        selected = pick_blocks(store_table, store_pick)
        predicted = jnp.einsum(
            "sar,skbr->skab", factor_rows, selected, preferred_element_type=jnp.float32
        )
        misfit = (predicted - measured.astype(jnp.float32)).astype(jnp.bfloat16)
        return (misfit, selected)

    def first_pass(running, inputs_now):
        factor_rows, measured, store_pick, alive = inputs_now
        misfit, selected = misfit_of(factor_rows, measured, store_pick, group_low)
        partial_value = jnp.einsum(
            "skab,sar->skbr", misfit, factor_rows, preferred_element_type=jnp.float32
        )
        selector = one_hot_of(store_pick, group_count) * alive[:, None, None].astype(jnp.bfloat16)
        selector = selector.reshape(-1, group_count)
        added = sum_into_blocks(selector, partial_value.reshape(-1, block_len, rank_len))
        return (running + added.reshape(running.shape), None)

    store_grad, _ = lax.scan(first_pass, jnp.zeros(group_low.shape, jnp.float32), input_arrays)
    own_grad = lax.psum_scatter(
        store_grad.astype(jnp.bfloat16), "col", scatter_dimension=0, tiled=True
    ).astype(jnp.float32)
    new_store = own_store - learn_rate * (own_grad + weight_decay * own_store)
    new_low = lax.all_gather(new_store.astype(jnp.bfloat16), "col", axis=0, tiled=True)

    def second_pass(running, inputs_now):
        factor_rows, measured, store_pick, alive = inputs_now
        misfit, selected = misfit_of(factor_rows, measured, store_pick, new_low)
        partial_value = jnp.einsum(
            "skab,skbr->sar", misfit, selected, preferred_element_type=jnp.float32
        )
        return (running, partial_value * alive[:, None, None])

    _, sku_terms = lax.scan(second_pass, jnp.zeros((), jnp.float32), input_arrays)
    sku_terms = sku_terms.reshape(rows_per_owner, owner_wise, block_len, rank_len)
    arrived, requested = (
        lax.all_to_all(
            sku_terms.astype(jnp.bfloat16), "row", split_axis=0, concat_axis=0, tiled=True
        ).astype(sku_terms.dtype),
        lax.all_to_all(requested_ids, "row", split_axis=0, concat_axis=0, tiled=True),
    )
    owner_selector = one_hot_of(requested.reshape(-1), own_sku.shape[0])
    sku_grad = sum_into_blocks(owner_selector, arrived.reshape(-1, block_len, rank_len)).reshape(
        own_sku.shape
    )
    new_sku = own_sku - learn_rate * (sku_grad + weight_decay * own_sku)
    return (new_sku.reshape(sku_factors.shape), new_store.reshape(store_factors.shape))


def solution(mesh):
    placed = (
        P(("row", "col"), None, None, None),
        P(("row", "col")),
        P(("row", "col"), None),
        P("row", "col", None),
        P(("row", "col"), None),
        P(("row", "col"), None),
    )
    return jax.shard_map(
        local,
        mesh=mesh,
        in_specs=placed,
        out_specs=(P(("row", "col"), None), P(("row", "col"), None)),
        check_vma=False,
    )
```

profile of v0, /device:TPU:1, one launch (start us, length us, event | category | flops | bytes accessed | tf_op | source)
XLA Modules:
  0.0 615.1 jit_solution(6437054069210750327)
XLA Ops:
  7.2 2.7 convert_element_type.96
  12.4 12.0 %copy.26 = bf16[32,8,128,128]{2,3,1,0:T(8,128)(2,1)} copy(bf16[32,8,128,128]{3,2,1,0:T(8,128)(2,1)} %param.10) | data formatting | bytes 16777216 | tf_op args[0]
  25.1 38.6 %all-gather.6.cloned.1.call-done = bf16[128,128,256]{2,1,0:T(8,128)(2,1)} async-done(((bf16[16,128,256]{2,1,0:T(8,128)(2,1)}), bf16[128,128,256]{2,1,0:T(8,128)(2,1)}) %all-gather.6.cloned.1.call-update) | async-done | bytes 8388624 | tf_op jit(solution)/shard_map/all_gather | solution.py:47
  63.7 12.3 %copy.38 = bf16[16,8,128,256]{3,1,2,0:T(8,128)(2,1)} copy(bf16[16,8,128,256]{3,2,1,0:T(8,128)(2,1)} %bitcast.187) | data formatting | bytes 16777216
  76.0 4.8 convolution_convert_fusion.2
  81.3 41.4 %all-gather.4.cloned.1.call-done = bf16[80,128,256]{2,1,0:T(8,128)(2,1)} async-done(((bf16[5,128,256]{2,1,0:T(8,128)(2,1)}), bf16[80,128,256]{2,1,0:T(8,128)(2,1)}) %all-gather.4.cloned.1.call-update) | async-done | bytes 5242896 | tf_op jit(solution)/shard_map/all_gather | solution.py:50
  122.7 230.6 %while.22 = (s32[]{:T(128)}, f32[80,128,256]{2,1,0:T(8,128)}, s32[4,8,8]{2,1,0:T(8,128)S(1)}, bf16[4,8]{1,0:T(4,128)(2,1)S(1)}, bf16[80,128,256]{2,1,0:T(8,128)(...) while((s32[]{:T(128)}, f32[80,128,256]{2,1,0:T(8,128)}, ...), condition=%wide.region_1.2_spmd.clone, body=%wide.region_0.1_spmd.clone.sunk | while | flops 2101896192 | bytes 161484752 | solution.py:83
  137.1 5.8 copy.84
  143.0 3.3 convolution_convert_fusion.6
  146.3 8.8 %fusion.141 = (bf16[8,8,128,256]{3,2,1,0:T(8,128)(2,1)}, bf16[8,8,128,256]{3,2,1,0:T(8,128)(2,1)}) fusion(bf16[4,8,128,256]{3,2,1,0:T(8,128)(2,1)S(1)} %get-tuple-element.291, s32[]{:T(128)} %get-tuple-element.277, bf16[8,8,128,256]{3,1,2,0:T(8,128)(2,1)} %bitcast.177, bf16[4,8,8,128,128]{3,4,2,1,0:T(8,128)(2,1)} %get-tuple-element.292), kind=kOutput, calls=%fused_computation.25.clone.1 | convolution fusion | flops 1085276160 | bytes 15730176 | tf_op jit(solution)/shard_map/while/body/eval_jaxpr/skab,sar->skbr/dot_general | solution.py:75
  155.1 4.7 copy.85
  159.9 1.6 fusion.144
  162.1 4.7 copy.86
  166.8 3.9 convolution_add_fusion.3
  170.6 7.1 %copy.87 = f32[10,8,128,256]{3,2,1,0:T(8,128)} copy(f32[10,8,128,256]{3,1,2,0:T(8,128)S(1)} %bitcast.174) | data formatting | bytes 20971520 | tf_op jit(solution)/shard_map/while
  177.7 11.1 %bitcast_add_fusion.2 = f32[80,128,256]{2,1,0:T(8,128)} fusion(f32[10,8,128,256]{3,2,1,0:T(8,128)} %copy.87, f32[80,128,256]{2,1,0:T(8,128)} %get-tuple-element.278, pred[]{:T(512)S(6)} %compare.5), kind=kLoop, calls=%fused_computation.23.clone.1 | loop fusion | flops 5242880 | bytes 31457280 | tf_op jit(solution)/shard_map/while/body/eval_jaxpr/add | solution.py:81
  189.0 5.8 copy.84
  194.8 3.3 convolution_convert_fusion.6
  198.1 8.8 %fusion.141 = (bf16[8,8,128,256]{3,2,1,0:T(8,128)(2,1)}, bf16[8,8,128,256]{3,2,1,0:T(8,128)(2,1)}) fusion(bf16[4,8,128,256]{3,2,1,0:T(8,128)(2,1)S(1)} %get-tuple-element.291, s32[]{:T(128)} %get-tuple-element.277, bf16[8,8,128,256]{3,1,2,0:T(8,128)(2,1)} %bitcast.177, bf16[4,8,8,128,128]{3,4,2,1,0:T(8,128)(2,1)} %get-tuple-element.292), kind=kOutput, calls=%fused_computation.25.clone.1 | convolution fusion | flops 1085276160 | bytes 15730176 | tf_op jit(solution)/shard_map/while/body/eval_jaxpr/skab,sar->skbr/dot_general | solution.py:75
  206.9 4.7 copy.85
  211.7 1.6 fusion.144
  213.9 4.7 copy.86
  218.6 3.9 convolution_add_fusion.3
  222.4 7.1 %copy.87 = f32[10,8,128,256]{3,2,1,0:T(8,128)} copy(f32[10,8,128,256]{3,1,2,0:T(8,128)S(1)} %bitcast.174) | data formatting | bytes 20971520 | tf_op jit(solution)/shard_map/while
  229.5 14.1 %bitcast_add_fusion.2 = f32[80,128,256]{2,1,0:T(8,128)} fusion(f32[10,8,128,256]{3,2,1,0:T(8,128)} %copy.87, f32[80,128,256]{2,1,0:T(8,128)} %get-tuple-element.278, pred[]{:T(512)S(6)} %compare.5), kind=kLoop, calls=%fused_computation.23.clone.1 | loop fusion | flops 5242880 | bytes 31457280 | tf_op jit(solution)/shard_map/while/body/eval_jaxpr/add | solution.py:81
  243.7 5.8 copy.84
  249.6 3.3 convolution_convert_fusion.6
  252.9 8.8 %fusion.141 = (bf16[8,8,128,256]{3,2,1,0:T(8,128)(2,1)}, bf16[8,8,128,256]{3,2,1,0:T(8,128)(2,1)}) fusion(bf16[4,8,128,256]{3,2,1,0:T(8,128)(2,1)S(1)} %get-tuple-element.291, s32[]{:T(128)} %get-tuple-element.277, bf16[8,8,128,256]{3,1,2,0:T(8,128)(2,1)} %bitcast.177, bf16[4,8,8,128,128]{3,4,2,1,0:T(8,128)(2,1)} %get-tuple-element.292), kind=kOutput, calls=%fused_computation.25.clone.1 | convolution fusion | flops 1085276160 | bytes 15730176 | tf_op jit(solution)/shard_map/while/body/eval_jaxpr/skab,sar->skbr/dot_general | solution.py:75
  261.7 4.7 copy.85
  268.7 4.7 copy.86
  273.3 3.9 convolution_add_fusion.3
  277.2 7.1 %copy.87 = f32[10,8,128,256]{3,2,1,0:T(8,128)} copy(f32[10,8,128,256]{3,1,2,0:T(8,128)S(1)} %bitcast.174) | data formatting | bytes 20971520 | tf_op jit(solution)/shard_map/while
  284.3 14.1 %bitcast_add_fusion.2 = f32[80,128,256]{2,1,0:T(8,128)} fusion(f32[10,8,128,256]{3,2,1,0:T(8,128)} %copy.87, f32[80,128,256]{2,1,0:T(8,128)} %get-tuple-element.278, pred[]{:T(512)S(6)} %compare.5), kind=kLoop, calls=%fused_computation.23.clone.1 | loop fusion | flops 5242880 | bytes 31457280 | tf_op jit(solution)/shard_map/while/body/eval_jaxpr/add | solution.py:81
  298.5 5.8 copy.84
  304.4 3.3 convolution_convert_fusion.6
  307.7 8.8 %fusion.141 = (bf16[8,8,128,256]{3,2,1,0:T(8,128)(2,1)}, bf16[8,8,128,256]{3,2,1,0:T(8,128)(2,1)}) fusion(bf16[4,8,128,256]{3,2,1,0:T(8,128)(2,1)S(1)} %get-tuple-element.291, s32[]{:T(128)} %get-tuple-element.277, bf16[8,8,128,256]{3,1,2,0:T(8,128)(2,1)} %bitcast.177, bf16[4,8,8,128,128]{3,4,2,1,0:T(8,128)(2,1)} %get-tuple-element.292), kind=kOutput, calls=%fused_computation.25.clone.1 | convolution fusion | flops 1085276160 | bytes 15730176 | tf_op jit(solution)/shard_map/while/body/eval_jaxpr/skab,sar->skbr/dot_general | solution.py:75
  316.5 4.7 copy.85
  323.5 4.7 copy.86
  328.1 3.9 convolution_add_fusion.3
  332.0 7.1 %copy.87 = f32[10,8,128,256]{3,2,1,0:T(8,128)} copy(f32[10,8,128,256]{3,1,2,0:T(8,128)S(1)} %bitcast.174) | data formatting | bytes 20971520 | tf_op jit(solution)/shard_map/while
  339.1 14.1 %bitcast_add_fusion.2 = f32[80,128,256]{2,1,0:T(8,128)} fusion(f32[10,8,128,256]{3,2,1,0:T(8,128)} %copy.87, f32[80,128,256]{2,1,0:T(8,128)} %get-tuple-element.278, pred[]{:T(512)S(6)} %compare.5), kind=kLoop, calls=%fused_computation.23.clone.1 | loop fusion | flops 5242880 | bytes 31457280 | tf_op jit(solution)/shard_map/while/body/eval_jaxpr/add | solution.py:81
  353.2 7.1 %convert_element_type.99 = bf16[80,128,256]{2,1,0:T(8,128)(2,1)} convert(f32[80,128,256]{2,1,0:T(8,128)} %get-tuple-element.76) | non-fusion elementwise | flops 2621440 | bytes 15728640 | tf_op jit(solution)/shard_map/convert_element_type | solution.py:85
  360.4 78.1 %reduce-scatter.4.cloned.1.call-done = bf16[5,128,256]{2,1,0:T(8,128)(2,1)} async-done(((bf16[80,128,256]{2,1,0:T(8,128)(2,1)}), bf16[5,128,256]{2,1,0:T(8,128)(2,1)}) %reduce-scatter.4.cloned.1.call-update) | async-done | bytes 327696
  438.5 2.0 fusion.88
  441.2 6.0 all-to-all-start
  447.2 50.2 %all-gather.8.cloned.1.call-done = bf16[80,128,256]{2,1,0:T(8,128)(2,1)} async-done(((bf16[5,128,256]{2,1,0:T(8,128)(2,1)}), bf16[80,128,256]{2,1,0:T(8,128)(2,1)}) %all-gather.8.cloned.1.call-update) | async-done | bytes 5242896 | tf_op jit(solution)/shard_map/all_gather | solution.py:88
  497.5 69.7 %while.21 = (s32[]{:T(128)}, bf16[4,8,128,256]{3,2,1,0:T(8,128)(2,1)}, s32[4,8,8]{2,1,0:T(8,128)S(1)}, bf16[80,128,256]{2,1,0:T(8,128)(2,1)}, bf16[4,8,128,256]{...) while((s32[]{:T(128)}, ...), condition=%wide.region_4.5_spmd, body=%wide.region_3.4_spmd.sunk | while | flops 1414796288 | bytes 31985052 | solution.py:98
  497.5 5.8 copy.82
  503.4 3.2 convolution_convert_fusion.5
  507.3 7.6 %fusion.131 = bf16[4,8,128,256]{3,2,1,0:T(8,128)(2,1)} fusion(bf16[4,8,128,256]{3,2,1,0:T(8,128)(2,1)} %get-tuple-element.304, s32[]{:T(128)} %get-tuple-element.303, bf16[8,8,128,256]{3,1,2,0:T(8,128)(2,1)} %bitcast.182, bf16[4,8,8,128,128]{3,4,2,1,0:T(8,128)(2,1)} %get-tuple-element.316, f32[8]{0:T(128)S(1)} %fusion.130, ...), kind=kOutput, calls=%fused_computation.12.clone.1 | convolution fusion | flops 1077149696 | bytes 12060672 | tf_op jit(solution)/shard_map/while/body/eval_jaxpr/skab,skbr->sar/dot_general | solution.py:93
  515.0 5.8 copy.82
  520.8 3.2 convolution_convert_fusion.5
  524.7 7.6 %fusion.131 = bf16[4,8,128,256]{3,2,1,0:T(8,128)(2,1)} fusion(bf16[4,8,128,256]{3,2,1,0:T(8,128)(2,1)} %get-tuple-element.304, s32[]{:T(128)} %get-tuple-element.303, bf16[8,8,128,256]{3,1,2,0:T(8,128)(2,1)} %bitcast.182, bf16[4,8,8,128,128]{3,4,2,1,0:T(8,128)(2,1)} %get-tuple-element.316, f32[8]{0:T(128)S(1)} %fusion.130, ...), kind=kOutput, calls=%fused_computation.12.clone.1 | convolution fusion | flops 1077149696 | bytes 12060672 | tf_op jit(solution)/shard_map/while/body/eval_jaxpr/skab,skbr->sar/dot_general | solution.py:93
  532.4 5.8 copy.82
  538.2 3.2 convolution_convert_fusion.5
  542.1 7.6 %fusion.131 = bf16[4,8,128,256]{3,2,1,0:T(8,128)(2,1)} fusion(bf16[4,8,128,256]{3,2,1,0:T(8,128)(2,1)} %get-tuple-element.304, s32[]{:T(128)} %get-tuple-element.303, bf16[8,8,128,256]{3,1,2,0:T(8,128)(2,1)} %bitcast.182, bf16[4,8,8,128,128]{3,4,2,1,0:T(8,128)(2,1)} %get-tuple-element.316, f32[8]{0:T(128)S(1)} %fusion.130, ...), kind=kOutput, calls=%fused_computation.12.clone.1 | convolution fusion | flops 1077149696 | bytes 12060672 | tf_op jit(solution)/shard_map/while/body/eval_jaxpr/skab,skbr->sar/dot_general | solution.py:93
  549.8 5.8 copy.82
  555.7 3.2 convolution_convert_fusion.5
  559.6 7.6 %fusion.131 = bf16[4,8,128,256]{3,2,1,0:T(8,128)(2,1)} fusion(bf16[4,8,128,256]{3,2,1,0:T(8,128)(2,1)} %get-tuple-element.304, s32[]{:T(128)} %get-tuple-element.303, bf16[8,8,128,256]{3,1,2,0:T(8,128)(2,1)} %bitcast.182, bf16[4,8,8,128,128]{3,4,2,1,0:T(8,128)(2,1)} %get-tuple-element.316, f32[8]{0:T(128)S(1)} %fusion.130, ...), kind=kOutput, calls=%fused_computation.12.clone.1 | convolution fusion | flops 1077149696 | bytes 12060672 | tf_op jit(solution)/shard_map/while/body/eval_jaxpr/skab,skbr->sar/dot_general | solution.py:93
  567.2 4.9 all-to-all-start.1
  572.8 25.6 %all-to-all-done.1 = bf16[8,4,128,256]{3,2,1,0:T(8,128)(2,1)S(1)} async-done(((bf16[8,4,128,256]{3,2,1,0:T(8,128)(2,1)}), bf16[8,4,128,256]{3,2,1,0:T(8,128)(2,1)S(1)}, u32[]{:S(2)}, u32[]{:S(2)}) %all-to-all-start.1) | async-done | bytes 2097184 | tf_op jit(solution)/shard_map/all_to_all | solution.py:101
  600.2 2.0 convolution_add_fusion.1
  602.2 2.7 reshape.197
  605.0 3.2 multiply_subtract_fusion
  (80 shorter events, 15.8 us)
Async XLA Ops:
  7.2 2.9 copy-start.2
  7.2 4.2 copy-start.7
  7.2 56.5 %all-gather.6.cloned.1.call-start = ((), (), s32[]{:S(2)}) async-start(), calls=%async_computation.4 | async-start | bytes 9437184 | tf_op jit(solution)/shard_map/all_gather | solution.py:47
  10.0 112.7 %all-gather.4.cloned.1.call-start = ((), (), s32[]{:S(2)}) async-start(), calls=%async_computation.3 | async-start | bytes 5570560 | tf_op jit(solution)/shard_map/all_gather | solution.py:50
  10.8 427.6 %reduce-scatter.4.cloned.1.call-start = ((), (), s32[]{:S(2)}) async-start(), calls=%async_computation.6 | async-start | bytes 5570560
  12.4 12.0 %copy-start.4 = (s32[32,8]{0,1:T(8,128)S(1)}, s32[32,8]{0,1:T(8,128)}, u32[]{:S(2)}) copy-start(s32[32,8]{0,1:T(8,128)} %param.12) | copy-start | bytes 3076
  12.4 12.1 %copy-start.5 = (s32[32]{0:T(128)S(1)}, s32[32]{0:T(128)}, u32[]{:S(2)}) copy-start(s32[32]{0:T(128)} %param.11) | copy-start | bytes 388
  159.9 2.2 copy-start
  211.7 2.2 copy-start
  266.5 2.2 copy-start
  321.3 2.2 copy-start
  360.3 78.2 %copy-start.3 = (f32[640,256]{1,0:T(8,128)S(1)}, f32[640,256]{1,0:T(8,128)}, u32[]{:S(2)}) copy-start(f32[640,256]{1,0:T(8,128)} %param.15) | copy-start | bytes 1966084
  360.3 80.2 %copy-start.6 = (s32[32]{0:T(128)S(1)}, s32[32]{0:T(128)}, u32[]{:S(2)}) copy-start(s32[32]{0:T(128)} %param.11) | copy-start | bytes 388
  360.3 137.1 %all-gather.8.cloned.1.call-start = ((), (), s32[]{:S(2)}) async-start(), calls=%async_computation.5 | async-start | bytes 5570560 | tf_op jit(solution)/shard_map/all_gather | solution.py:88
  441.2 126.0 %all-to-all-start = ((s32[8,1,4]{2,1,0:T(1,128)}), s32[8,1,4]{2,1,0:T(1,128)S(1)}, u32[]{:S(2)}, u32[]{:S(2)}) async-start(s32[8,1,4]{2,1,0:T(1,128)} %bitcast.10), calls=%async_computation | async-start | bytes 8192 | tf_op jit(solution)/shard_map/all_to_all | solution.py:104
  567.2 31.3 %all-to-all-start.1 = ((bf16[8,4,128,256]{3,2,1,0:T(8,128)(2,1)}), bf16[8,4,128,256]{3,2,1,0:T(8,128)(2,1)S(1)}, u32[]{:S(2)}, u32[]{:S(2)}) async-start(bf16[8,4,128,256]{3,2,1,0:T(8,128)(2,1)} %bitcast.193), calls=%async_computation.1 | async-start | bytes 4194304 | tf_op jit(solution)/shard_map/all_to_all | solution.py:101
  600.2 4.8 copy-start.1
Sparse Core Ops, SparseCore 0:
  10.3 53.3 all-gather.5
  66.4 56.2 all-gather.3
  360.5 77.9 reduce-scatter.3
  440.7 56.7 all-gather.7
where the time goes:
time: 623 us; the launch traced here: 615 us
  waiting for transfers between devices  234 us (38%)
  local copies, waits for them, and re-layouts  149 us (24%)
  matrix products  121 us (19%)
  other arithmetic  71.3 us (11%)
  loops' own time  14.6 us (2%)
  between operations  14.2 us (2%)
  starting transfers between devices  11.1 us (2%)
    while x28, local copies, waits for them, and re-layouts  115 us
    unnamed x5, waiting for transfers between devices  78.1 us
    add x4, other arithmetic, first_pass(): return (running + added.reshape(running.shape), None)  53.5 us
    all_gather x1, waiting for transfers between devices, local(): lax.all_gather(new_store.astype(jnp.bfloat16), 'col', axis=0, tiled=True)  50.2 us
    all_gather x1, waiting for transfers between devices, local(): lax.all_gather(own_store.astype(jnp.bfloat16), 'col', axis=0, tiled=True)  41.4 us
    all_gather x1, waiting for transfers between devices, local(): all_tables = lax.all_gather(own_table, 'row', axis=0, tiled=True)  38.6 us
    dot_general x4, matrix products, first_pass(): jnp.einsum('skab,sar->skbr', misfit, factor_rows, preferred_element_type=...  35.2 us
    dot_general x9, matrix products, pick_blocks(): jnp.dot(selector, flat_table, preferred_element_type=jnp.float32)  31.1 us
  transfers between devices with their start and end apart: 6, of which 5 were waited for; matrix products, arithmetic and copies ran while one was open for 17% of the time, Pallas kernels for 0%

commit v1 on v0

v1 whole, which is shorter than its diff:
```python
import jax
import jax.numpy as jnp
from jax import lax
from jax.experimental import pallas as pl
from jax.experimental.pallas import tpu as pltpu
from jax.sharding import PartitionSpec as P

learn_rate = 0.01
weight_decay = 0.05
BS = 128
R = 256
K = 8
CAP = 4
N_ROW = 8
SLOTS = 32
UB = 16
VB = 5
VG = 80
DEPTH = 4
VMEM_MOST = 60 * 1024 * 1024

NT = (((1,), (1,)), ((), ()))
f32 = jnp.float32
bf16 = jnp.bfloat16


def live_list(counts, order):
    total = jnp.int32(0)
    for o in range(N_ROW):
        for t in range(CAP):
            order[total] = o * CAP + t
            total = total + (t < counts[o]).astype(jnp.int32)
    return total


def misfit_pair(x, store, first, second, obs, k):
    two = jnp.concatenate([store[first], store[second]], axis=0)
    predicted = lax.dot_general(x, two, NT, preferred_element_type=f32)
    measured = jnp.concatenate([obs[k], obs[k + 1]], axis=1)
    return (predicted - measured.astype(f32)).astype(bf16), two


def first_pass(ids, sku_ids, counts, tables, obs, store, out, acc, order, sku_buf, obs_buf, sem):
    total = live_list(counts, order)

    def copies(i):
        s = order[i]
        at = lax.rem(i, DEPTH)
        return (
            pltpu.make_async_copy(tables.at[s // CAP * UB + sku_ids[s]], sku_buf.at[at], sem.at[0, at]),
            pltpu.make_async_copy(obs.at[s], obs_buf.at[at], sem.at[1, at]),
        )

    for i in range(DEPTH - 1):

        @pl.when(i < total)
        def _():
            for c in copies(i):
                c.start()

    acc[...] = jnp.zeros_like(acc)

    @pl.loop(0, total)
    def _(i):
        @pl.when(i + DEPTH - 1 < total)
        def _():
            for c in copies(i + DEPTH - 1):
                c.start()

        for c in copies(i):
            c.wait()
        s = order[i]
        at = lax.rem(i, DEPTH)
        x = sku_buf[at]
        xt = x.T
        now = obs_buf.at[at]
        for k in range(0, K, 2):
            a, b = ids[s, k], ids[s, k + 1]
            misfit, _ = misfit_pair(x, store, a, b, now, k)
            g = jnp.dot(xt, misfit, preferred_element_type=f32)
            acc[a] += g[:, :BS]
            acc[b] += g[:, BS:]

    out[...] = acc[...].astype(bf16)


def second_pass(ids, sku_ids, counts, tables, obs, store, out, order, sku_buf, obs_buf, sem):
    total = live_list(counts, order)

    def copies(i):
        s = order[i]
        at = lax.rem(i, DEPTH)
        return (
            pltpu.make_async_copy(tables.at[s // CAP * UB + sku_ids[s]], sku_buf.at[at], sem.at[0, at]),
            pltpu.make_async_copy(obs.at[s], obs_buf.at[at], sem.at[1, at]),
        )

    for i in range(DEPTH - 1):

        @pl.when(i < total)
        def _():
            for c in copies(i):
                c.start()

    out[...] = jnp.zeros_like(out)

    @pl.loop(0, total)
    def _(i):
        @pl.when(i + DEPTH - 1 < total)
        def _():
            for c in copies(i + DEPTH - 1):
                c.start()

        for c in copies(i):
            c.wait()
        s = order[i]
        at = lax.rem(i, DEPTH)
        x = sku_buf[at]
        now = obs_buf.at[at]
        g = jnp.zeros((BS, R), f32)
        for k in range(0, K, 2):
            misfit, two = misfit_pair(x, store, ids[s, k], ids[s, k + 1], now, k)
            g = g + jnp.dot(misfit, two, preferred_element_type=f32)
        out[s] = g.astype(bf16)


def last_step(requested, arrived, own, out, acc):
    acc[...] = jnp.zeros_like(acc)

    @pl.loop(0, SLOTS)
    def _(q):
        acc[requested[q]] += arrived[q].astype(f32)

    out[...] = own[...] - learn_rate * (acc[...] + weight_decay * own[...])


SMEM = pl.BlockSpec(memory_space=pltpu.SMEM)
VMEM = pl.BlockSpec(memory_space=pltpu.VMEM)
ANY = pl.BlockSpec(memory_space=pl.ANY)
params = pltpu.CompilerParams(vmem_limit_bytes=VMEM_MOST)


def local(observed, sku_ids, store_ids, live_slot_counts, sku_factors, store_factors):
    counts = live_slot_counts.reshape(N_ROW)
    own_sku = sku_factors.reshape(UB, BS, R)
    own_store = store_factors.reshape(VB, BS, R)
    tables = lax.all_gather(own_sku.astype(bf16), "row", axis=0, tiled=True)
    group_low = lax.all_gather(own_store.astype(bf16), "col", axis=0, tiled=True)
    slot_bufs = [
        pltpu.SMEM((SLOTS + 1,), jnp.int32),
        pltpu.VMEM((DEPTH, BS, R), bf16),
        pltpu.VMEM((DEPTH, K, BS, BS), bf16),
        pltpu.SemaphoreType.DMA((2, DEPTH)),
    ]
    grad = pl.pallas_call(
        first_pass,
        out_shape=jax.ShapeDtypeStruct((VG, R, BS), bf16),
        in_specs=[SMEM, SMEM, SMEM, ANY, ANY, VMEM],
        out_specs=VMEM,
        scratch_shapes=[pltpu.VMEM((VG, R, BS), f32)] + slot_bufs,
        compiler_params=params,
        name="first_pass",
    )(store_ids, sku_ids, counts, tables, observed, group_low)
    own_grad = lax.psum_scatter(grad, "col", scatter_dimension=0, tiled=True).astype(f32)
    own_grad = own_grad.transpose(0, 2, 1)
    new_store = own_store - learn_rate * (own_grad + weight_decay * own_store)
    new_low = lax.all_gather(new_store.astype(bf16), "col", axis=0, tiled=True)
    terms = pl.pallas_call(
        second_pass,
        out_shape=jax.ShapeDtypeStruct((SLOTS, BS, R), bf16),
        in_specs=[SMEM, SMEM, SMEM, ANY, ANY, VMEM],
        out_specs=VMEM,
        scratch_shapes=slot_bufs,
        compiler_params=params,
        name="second_pass",
    )(store_ids, sku_ids, counts, tables, observed, new_low)
    arrived = lax.all_to_all(
        terms.reshape(N_ROW, CAP, BS, R), "row", split_axis=0, concat_axis=0, tiled=True
    )
    requested = lax.all_to_all(
        sku_ids.reshape(N_ROW, CAP), "row", split_axis=0, concat_axis=0, tiled=True
    )
    new_sku = pl.pallas_call(
        last_step,
        out_shape=jax.ShapeDtypeStruct((UB, BS, R), f32),
        in_specs=[SMEM, VMEM, VMEM],
        out_specs=VMEM,
        scratch_shapes=[pltpu.VMEM((UB, BS, R), f32)],
        compiler_params=params,
        name="last_step",
    )(requested.reshape(SLOTS), arrived.reshape(SLOTS, BS, R), own_sku)
    return new_sku.reshape(sku_factors.shape), new_store.reshape(store_factors.shape)


def solution(mesh):
    placed = (
        P(("row", "col"), None, None, None),
        P(("row", "col")),
        P(("row", "col"), None),
        P("row", "col", None),
        P(("row", "col"), None),
        P(("row", "col"), None),
    )
    return jax.shard_map(
        local,
        mesh=mesh,
        in_specs=placed,
        out_specs=(P(("row", "col"), None), P(("row", "col"), None)),
        check_vma=False,
    )
```

time: 623 us -> 353 us (0.57)
  local copies, waits for them, and re-layouts: 149 us -> 11.6 us
  matrix products: 121 us -> 0 us
  other arithmetic: 71.3 us -> 7.21 us
  Pallas kernels: 0 us -> 36.5 us
  waiting for transfers between devices: 234 us -> 269 us
  loops' own time: 14.6 us -> 0 us
    dot_general x27 -> x0, matrix products: 121 us -> none  [the longest x4 35.2 us: first_pass(): jnp.einsum('skab,sar->skbr', misfit, factor_rows, preferred_element_type=...]
    while x28 -> x0, local copies, waits for them, and re-layouts: 115 us -> none
    add x5 -> x0, other arithmetic: 53.5 us -> none  [the longest x4 53.5 us: first_pass(): return (running + added.reshape(running.shape), None)]
    pallas_call x0 -> x3, Pallas kernels: none -> 36.5 us  [the longest x1 18.9 us: local(): pl.pallas_call(first_pass, out_shape=jax.ShapeDtypeStruct((VG, R, BS), bf...]
    all_gather x3, waiting for transfers between devices: 130 us -> 161 us  [the longest x1 57.9 us: local(): lax.all_gather(own_store.astype(bf16), 'col', axis=0, tiled=True)]
    unnamed x20 -> x9, local copies, waits for them, and re-layouts: 26.7 us -> 2.02 us
    another operation x2 -> x0, loops' own time: 14.6 us -> none  [the longest x1 14.6 us: local(): lax.scan(first_pass, jnp.zeros(group_low.shape, jnp.float32), input_arrays)]
    pallas_call x0 -> x1, local copies, waits for them, and re-layouts: none -> 7.77 us  [local(): pl.pallas_call(first_pass, out_shape=jax.ShapeDtypeStruct((VG, R, BS), bf...]
  transfers between devices with their start and end apart: 6 -> 6, of which waited for: 5 -> 5; matrix products, arithmetic and copies ran while one was open for 17% -> 1% of each run, Pallas kernels for 0% -> 4%
where the time goes in v1:
time: 353 us; the launch traced here: 349 us
  waiting for transfers between devices  269 us (76%)
  Pallas kernels  36.5 us (10%)
  between operations  13.8 us (4%)
  local copies, waits for them, and re-layouts  11.6 us (3%)
  starting transfers between devices  10.8 us (3%)
  other arithmetic  7.21 us (2%)
    unnamed x5, waiting for transfers between devices  84.1 us
    all_gather x1, waiting for transfers between devices, local(): lax.all_gather(own_store.astype(bf16), 'col', axis=0, tiled=True)  57.9 us
    all_gather x1, waiting for transfers between devices, local(): tables = lax.all_gather(own_sku.astype(bf16), 'row', axis=0, tiled=True)  52 us
    all_gather x1, waiting for transfers between devices, local(): new_low = lax.all_gather(new_store.astype(bf16), 'col', axis=0, tiled=True)  50.7 us
    all_to_all x1, waiting for transfers between devices, local(): lax.all_to_all(terms.reshape(N_ROW, CAP, BS, R), 'row', split_axis=0, con...  24.5 us
    pallas_call x1, Pallas kernels, local(): pl.pallas_call(first_pass, out_shape=jax.ShapeDtypeStruct((VG, R, BS), bf...  18.9 us
    pallas_call x1, Pallas kernels, local(): pl.pallas_call(second_pass, out_shape=jax.ShapeDtypeStruct((SLOTS, BS, R)...  13.1 us
    pallas_call x1, local copies, waits for them, and re-layouts, local(): pl.pallas_call(first_pass, out_shape=jax.ShapeDtypeStruct((VG, R, BS), bf...  7.77 us
  transfers between devices with their start and end apart: 6, of which 5 were waited for; matrix products, arithmetic and copies ran while one was open for 1% of the time, Pallas kernels for 4%

profile of v1, /device:TPU:1, one launch (start us, length us, event | category | flops | bytes accessed | tf_op | source)
XLA Modules:
  0.0 349.2 jit_solution(10888578676238912411)
XLA Ops:
  7.2 0.0 copy-start.3
  7.2 0.0 all-gather.6.cloned.1.call-start
  7.2 1.8 convert_element_type.11
  9.1 0.0 all-gather.6.cloned.1.call-update
  9.1 0.0 all-gather.4.cloned.1.call-start
  9.1 2.7 convert_element_type.10
  11.8 0.0 all-gather.4.cloned.1.call-update
  11.9 0.0 reduce-scatter.4.cloned.1.call-start
  11.9 0.0 copy-done.3
  11.9 0.7 copy.17.ids
  12.6 57.9 %all-gather.6.cloned.1.call-done.store = bf16[80,128,256]{2,1,0:T(8,128)(2,1)} async-done(((bf16[5,128,256]{2,1,0:T(8,128)(2,1)}), bf16[80,128,256]{2,1,0:T(8,128)(2,1)}) %all-gather.6.cloned.1.call-update) | async-done | bytes 5242896 | tf_op jit(solution)/shard_map/all_gather | solution.py:148
  70.4 52.0 %all-gather.4.cloned.1.call-done.tables = bf16[128,128,256]{2,1,0:T(8,128)(2,1)} async-done(((bf16[16,128,256]{2,1,0:T(8,128)(2,1)}), bf16[128,128,256]{2,1,0:T(8,128)(2,1)}) %all-gather.4.cloned.1.call-update) | async-done | bytes 8388624 | tf_op jit(solution)/shard_map/all_gather | solution.py:147
  122.5 18.9 %first_pass.1 = bf16[80,256,128]{2,1,0:T(8,128)(2,1)} custom-call(s32[32,8]{1,0:T(8,128)} %copy.17.ids, s32[32]{0:T(128)} %sku_ids.3, s32[8]{0:T(128)} %bitcast.24, bf16[128,128,256]{2,1,0:T(8,128)(2,1)} %all-gather.4.cloned.1.call-done.tables, bf16[32,8,128,128]{3,2,1,0:T(8,128)(2,1)} %obs.3, bf16[80,128,256]{2,1,0:T(8,128)(2,1)} %all-gather.6.cloned.1.call-done.store), custom_call_target="tpu_custom_call" | custom-call | tf_op jit(solution)/shard_map/first_pass/pallas_call | solution.py:155
  141.4 7.8 %copy.16 = bf16[80,256,128]{1,2,0:T(8,128)(2,1)} copy(bf16[80,256,128]{2,1,0:T(8,128)(2,1)} %first_pass.1) | data formatting | bytes 10485760 | tf_op jit(solution)/shard_map/first_pass/pallas_call | solution.py:155
  149.2 0.0 copy-start.1
  149.2 0.0 copy-start.2
  149.2 0.0 reduce-scatter.4.cloned.1.call-update
  149.2 0.0 all-gather.8.cloned.1.call-start
  149.2 84.1 %reduce-scatter.4.cloned.1.call-done = bf16[5,256,128]{1,2,0:T(8,128)(2,1)} async-done(((bf16[80,256,128]{1,2,0:T(8,128)(2,1)}), bf16[5,256,128]{1,2,0:T(8,128)(2,1)}) %reduce-scatter.4.cloned.1.call-update) | async-done | bytes 327696
  233.3 0.0 copy-done.1
  233.3 2.0 fusion.2
  235.3 0.0 all-gather.8.cloned.1.call-update
  235.4 0.0 copy-done.2
  235.4 0.7 all_to_all.9
  236.0 6.0 %all-to-all-start = ((s32[8,1,4]{2,1,0:T(1,128)}), s32[8,1,4]{2,1,0:T(1,128)S(1)}, u32[]{:S(2)}, u32[]{:S(2)}) async-start(s32[8,1,4]{2,1,0:T(1,128)} %bitcast), calls=%async_computation | async-start | bytes 8192 | tf_op jit(solution)/shard_map/all_to_all | solution.py:180
  242.0 50.7 %all-gather.8.cloned.1.call-done.store = bf16[80,128,256]{2,1,0:T(8,128)(2,1)} async-done(((bf16[5,128,256]{2,1,0:T(8,128)(2,1)}), bf16[80,128,256]{2,1,0:T(8,128)(2,1)}) %all-gather.8.cloned.1.call-update) | async-done | bytes 5242896 | tf_op jit(solution)/shard_map/all_gather | solution.py:167
  292.7 13.1 %second_pass.1 = bf16[32,128,256]{2,1,0:T(8,128)(2,1)} custom-call(s32[32,8]{1,0:T(8,128)} %copy.17.ids, s32[32]{0:T(128)} %sku_ids.3, s32[8]{0:T(128)} %bitcast.25, bf16[128,128,256]{2,1,0:T(8,128)(2,1)} %all-gather.4.cloned.1.call-done.tables, bf16[32,8,128,128]{3,2,1,0:T(8,128)(2,1)} %obs.3, bf16[80,128,256]{2,1,0:T(8,128)(2,1)} %all-gather.8.cloned.1.call-done.store), custom_call_target="tpu_custom_call" | custom-call | tf_op jit(solution)/shard_map/second_pass/pallas_call | solution.py:168
  305.9 0.0 all-to-all-done
  305.9 4.6 %all-to-all-start.1 = ((bf16[8,4,128,256]{3,2,1,0:T(8,128)(2,1)}), bf16[8,4,128,256]{3,2,1,0:T(8,128)(2,1)S(1)}, u32[]{:S(2)}, u32[]{:S(2)}) async-start(bf16[8,4,128,256]{3,2,1,0:T(8,128)(2,1)} %bitcast.19), calls=%async_computation.1 | async-start | bytes 4194304 | tf_op jit(solution)/shard_map/all_to_all | solution.py:177
  310.5 0.6 broadcast.3
  311.1 0.6 reduce.3
  311.7 0.6 reshape.33.requested
  312.3 24.5 %all-to-all-done.1 = bf16[8,4,128,256]{3,2,1,0:T(8,128)(2,1)S(1)} async-done(((bf16[8,4,128,256]{3,2,1,0:T(8,128)(2,1)}), bf16[8,4,128,256]{3,2,1,0:T(8,128)(2,1)S(1)}, u32[]{:S(2)}, u32[]{:S(2)}) %all-to-all-start.1) | async-done | bytes 2097184 | tf_op jit(solution)/shard_map/all_to_all | solution.py:177
  336.8 0.0 copy-start
  336.8 1.3 copy-done
  338.2 4.5 %last_step.1 = f32[16,128,256]{2,1,0:T(8,128)} custom-call(s32[32]{0:T(128)} %reshape.33.requested, bf16[32,128,256]{2,1,0:T(8,128)(2,1)} %bitcast.18, f32[16,128,256]{2,1,0:T(8,128)} %bitcast.17), custom_call_target="tpu_custom_call" | custom-call | tf_op jit(solution)/shard_map/last_step/pallas_call | solution.py:183
Async XLA Ops:
  7.2 4.7 %copy-start.3 = (s32[32,8]{0,1:T(8,128)S(1)}, s32[32,8]{0,1:T(8,128)}, u32[]{:S(2)}) copy-start(s32[32,8]{0,1:T(8,128)} %param.8) | copy-start | bytes 3076
  7.2 63.3 %all-gather.6.cloned.1.call-start = ((), (), s32[]{:S(2)}) async-start(), calls=%async_computation.4 | async-start | bytes 5570560 | tf_op jit(solution)/shard_map/all_gather | solution.py:148
  9.1 113.4 %all-gather.4.cloned.1.call-start = ((), (), s32[]{:S(2)}) async-start(), calls=%async_computation.3 | async-start | bytes 9437184 | tf_op jit(solution)/shard_map/all_gather | solution.py:147
  11.9 221.4 %reduce-scatter.4.cloned.1.call-start = ((), (), s32[]{:S(2)}) async-start(), calls=%async_computation.6 | async-start | bytes 5570560
  149.2 84.1 %copy-start.1 = (f32[640,256]{1,0:T(8,128)S(1)}, f32[640,256]{1,0:T(8,128)}, u32[]{:S(2)}) copy-start(f32[640,256]{1,0:T(8,128)} %param.11) | copy-start | bytes 1966084
  149.2 86.2 %copy-start.2 = (s32[32]{0:T(128)S(1)}, s32[32]{0:T(128)}, u32[]{:S(2)}) copy-start(s32[32]{0:T(128)} %sku_ids.3) | copy-start | bytes 388
  149.2 143.5 %all-gather.8.cloned.1.call-start = ((), (), s32[]{:S(2)}) async-start(), calls=%async_computation.5 | async-start | bytes 5570560 | tf_op jit(solution)/shard_map/all_gather | solution.py:167
  236.0 69.8 %all-to-all-start = ((s32[8,1,4]{2,1,0:T(1,128)}), s32[8,1,4]{2,1,0:T(1,128)S(1)}, u32[]{:S(2)}, u32[]{:S(2)}) async-start(s32[8,1,4]{2,1,0:T(1,128)} %bitcast), calls=%async_computation | async-start | bytes 8192 | tf_op jit(solution)/shard_map/all_to_all | solution.py:180
  305.9 31.0 %all-to-all-start.1 = ((bf16[8,4,128,256]{3,2,1,0:T(8,128)(2,1)}), bf16[8,4,128,256]{3,2,1,0:T(8,128)(2,1)S(1)}, u32[]{:S(2)}, u32[]{:S(2)}) async-start(bf16[8,4,128,256]{3,2,1,0:T(8,128)(2,1)} %bitcast.19), calls=%async_computation.1 | async-start | bytes 4194304 | tf_op jit(solution)/shard_map/all_to_all | solution.py:177
  336.8 1.3 copy-start
Sparse Core Ops, SparseCore 0:
  10.7 59.6 all-gather.5
  72.7 49.6 all-gather.3
  149.3 83.9 reduce-scatter.3
  235.9 56.8 all-gather.7

commit v2 on v1

v2 whole, which is shorter than its diff:
```python
import jax
import jax.numpy as jnp
from jax import lax
from jax.experimental import pallas as pl
from jax.experimental.pallas import tpu as pltpu
from jax.sharding import PartitionSpec as P

learn_rate = 0.01
weight_decay = 0.05
BS = 128
R = 256
K = 8
CAP = 4
N_ROW = 8
SLOTS = 32
UB = 16
VB = 5
VG = 80
DEPTH = 4
VMEM_MOST = 60 * 1024 * 1024

RING = 4
MESH = pl.DeviceIdType.MESH
NT = (((1,), (1,)), ((), ()))
f32 = jnp.float32
bf16 = jnp.bfloat16


def live_list(counts, order):
    total = jnp.int32(0)
    for o in range(N_ROW):
        for t in range(CAP):
            order[total] = o * CAP + t
            total = total + (t < counts[o]).astype(jnp.int32)
    return total


def misfit_pair(x, store, first, second, obs, k):
    two = jnp.concatenate([store[first], store[second]], axis=0)
    predicted = lax.dot_general(x, two, NT, preferred_element_type=f32)
    measured = jnp.concatenate([obs[k], obs[k + 1]], axis=1)
    return (predicted - measured.astype(f32)).astype(bf16), two


def first_pass(ids, counts, fetched, obs, store, out, acc, order, sku_buf, obs_buf, sem):
    total = live_list(counts, order)

    def copies(i):
        s = order[i]
        at = lax.rem(i, DEPTH)
        return (
            pltpu.make_async_copy(fetched.at[lax.div(s, CAP), lax.rem(s, CAP)], sku_buf.at[at], sem.at[0, at]),
            pltpu.make_async_copy(obs.at[s], obs_buf.at[at], sem.at[1, at]),
        )

    for i in range(DEPTH - 1):

        @pl.when(i < total)
        def _():
            for c in copies(i):
                c.start()

    acc[...] = jnp.zeros_like(acc)

    @pl.loop(0, total)
    def _(i):
        @pl.when(i + DEPTH - 1 < total)
        def _():
            for c in copies(i + DEPTH - 1):
                c.start()

        for c in copies(i):
            c.wait()
        s = order[i]
        at = lax.rem(i, DEPTH)
        x = sku_buf[at]
        xt = x.T
        now = obs_buf.at[at]
        for k in range(0, K, 2):
            a, b = ids[s, k], ids[s, k + 1]
            misfit, _ = misfit_pair(x, store, a, b, now, k)
            g = jnp.dot(xt, misfit, preferred_element_type=f32)
            acc[a] += g[:, :BS]
            acc[b] += g[:, BS:]

    out[...] = acc[...].astype(bf16)


class Place:
    def __init__(self):
        self.row, self.col = lax.axis_index("row"), lax.axis_index("col")
        self.x, self.core = lax.div(self.row, 2), lax.rem(self.row, 2)
        self.z, self.y = lax.div(self.col, RING), lax.rem(self.col, RING)

    def row_of(self, dx, dc):
        return lax.rem(self.x + dx + RING, RING) * 2 + (1 - self.core if dc else self.core)

    def col_of(self, dy, dz):
        return lax.rem(self.z + dz + RING, RING) * RING + lax.rem(self.y + dy + RING, RING)

    def along_row(self, dx, dc):
        return (self.row_of(dx, dc), self.col)

    def along_col(self, dy, dz):
        return (self.row, self.col_of(dy, dz))


class Wire:
    def __init__(self, send_sem, recv_sem):
        self.send_sem, self.recv_sem, self.made = send_sem, recv_sem, []

    def copy(self, src, dst, to):
        n = len(self.made)
        c = pltpu.make_async_remote_copy(
            src, dst, self.send_sem.at[n], self.recv_sem.at[n], device_id=to, device_id_type=MESH
        )
        c.start()
        self.made.append(c)
        return c

    def finish(self):
        for c in self.made:
            c.wait_send()


def meet(peers):
    barrier = pltpu.get_barrier_semaphore()
    for p in peers:
        pl.semaphore_signal(barrier, inc=1, device_id=p, device_id_type=MESH)
    pl.semaphore_wait(barrier, len(peers))


def col_peers(me):
    return [me.along_col(d, 0) for d in (1, -1)] + [me.along_col(0, d) for d in (1, -1)]


PLACES = [(2, 0), (2, 1), (1, 0), (-1, 0), (1, 1), (-1, 1), (0, 1), (0, 0)]
QUARTER = BS // 4


class Gather:
    def __init__(self, me, wire, own, table):
        self.me, self.wire, self.table = me, wire, table
        self.first, self.second = {}, {}
        for d in (1, -1):
            for h in (0, 1):
                self.first[h, d] = self.send(own, (0, 0), h, 0, 2, self.step(h, 0, d))
        for d in (1, -1):
            for h in (0, 1):
                self.second[h, d, 0, 0] = self.send(own, (0, 0), h, 0, 2, self.step(h, 1, d))

    def step(self, h, phase, d):
        return (d, 0) if h == phase else (0, d)

    def at(self, ref, whole, offset, h, q, n):
        rows = pl.ds((2 * h + q) * QUARTER, n * QUARTER)
        if not whole:
            return ref.at[:, rows, :]
        return ref.at[pl.ds(self.me.col_of(*offset) * VB, VB), rows, :]

    def send(self, own, offset, h, q, n, to):
        src = self.at(own, False, offset, h, q, n) if own is not None else self.at(self.table, True, offset, h, q, n)
        return self.wire.copy(src, self.at(self.table, True, offset, h, q, n), self.me.along_col(*to))

    def middle(self):
        opposite = {}
        for d in (1, -1):
            for h in (0, 1):
                self.first[h, d].wait_recv()
                offset = self.step(h, 0, -d)
                q = 0 if d == 1 else 1
                opposite[h, d] = self.send(None, offset, h, q, 1, self.step(h, 0, d))
                for e in (1, -1):
                    self.second[h, e, -d, 0] = self.send(None, offset, h, 0, 2, self.step(h, 1, e))
        for d in (1, -1):
            for h in (0, 1):
                opposite[h, d].wait_recv()
                q = 0 if d == 1 else 1
                for e in (1, -1):
                    self.second[h, e, 2, q] = self.send(
                        None, self.step(h, 0, 2), h, q, 1, self.step(h, 1, e)
                    )

    def end(self):
        last = []
        for f in (0, -1, 1, 2):
            for e in (1, -1):
                for h in (0, 1):
                    if f == 2:
                        self.second[h, e, 2, 0].wait_recv()
                        self.second[h, e, 2, 1].wait_recv()
                    else:
                        self.second[h, e, f, 0].wait_recv()
                    a, b = self.step(h, 0, f), self.step(h, 1, -e)
                    q = 0 if e == 1 else 1
                    last.append(self.send(None, (a[0] + b[0], a[1] + b[1]), h, q, 1, self.step(h, 1, e)))
        for c in last:
            c.wait_recv()


class Exchange:
    def __init__(self, me, wire, send, recv, relay):
        self.me, self.wire, self.send, self.recv, self.relay = me, wire, send, recv, relay
        self.legs, self.got = {}, []

    def start(self, j):
        dx, dc = PLACES[j]
        me = self.me
        if dx == 2:
            for way, d in ((0, 1), (1, -1)):
                self.legs[way, dc] = self.wire.copy(
                    self.send.at[j, pl.ds(2 * way, 2)], self.relay.at[way, dc], me.along_row(d, 0)
                )
        elif (dx, dc) != (0, 0):
            self.got.append(
                self.wire.copy(self.send.at[j], self.recv.at[me.row], me.along_row(dx, dc))
            )

    def forward(self):
        me = self.me
        for dc in (0, 1):
            for way, d in ((0, 1), (1, -1)):
                self.legs[way, dc].wait_recv()
                self.got.append(
                    self.wire.copy(
                        self.relay.at[way, dc],
                        self.recv.at[me.row_of(-d, 0), pl.ds(2 * way, 2)],
                        me.along_row(d, dc),
                    )
                )

    def end(self):
        for c in self.got:
            c.wait_recv()


GATHER_COPIES = 44
EXCHANGE_COPIES = 13


def gather_kernel(
    ids, own_sku, own_store, group, fetched, requests,
    sku_v, store_v, low, send, relay, heard, heard_s, sems, send_sem, recv_sem,
):
    me = Place()
    load_store = pltpu.make_async_copy(own_store, store_v, sems.at[0])
    load_sku = pltpu.make_async_copy(own_sku, sku_v, sems.at[1])
    load_store.start()
    load_sku.start()
    peers = [me.along_row(*p) for p in PLACES[:-1]]
    meet(col_peers(me) + peers)
    wire = Wire(send_sem, recv_sem)
    asked = [
        wire.copy(ids.at[me.row_of(*p)], heard.at[me.row], me.along_row(*p)) for p in PLACES[:-1]
    ]
    own_ids = pltpu.make_async_copy(ids.at[me.row], heard.at[me.row], sems.at[2])
    own_ids.start()
    load_store.wait()
    low[...] = store_v[...].astype(bf16)
    gather = Gather(me, wire, low, group)
    keep_low = pltpu.make_async_copy(low, group.at[pl.ds(me.col * VB, VB)], sems.at[3])
    keep_low.start()
    for c in asked:
        c.wait_recv()
    own_ids.wait()
    to_scalars = pltpu.make_async_copy(heard, heard_s, sems.at[4])
    to_scalars.start()
    to_result = pltpu.make_async_copy(heard, requests, sems.at[5])
    to_result.start()
    load_sku.wait()
    to_scalars.wait()
    exchange = Exchange(me, wire, send, fetched, relay)
    for j, p in enumerate(PLACES):
        for t in range(CAP):
            send[j, t] = sku_v[heard_s[me.row_of(*p), 0, t]].astype(bf16)
        exchange.start(j)
    keep_sku = pltpu.make_async_copy(send.at[len(PLACES) - 1], fetched.at[me.row], sems.at[6])
    keep_sku.start()
    gather.middle()
    exchange.forward()
    gather.end()
    exchange.end()
    keep_low.wait()
    keep_sku.wait()
    to_result.wait()
    wire.finish()


def quarter(q):
    return pl.ds(q * (R // 4), R // 4)


class Sum:
    def __init__(self, me, wire, part, own_sum, far, near, far2, near2):
        self.me, self.wire, self.part, self.own_sum = me, wire, part, own_sum
        self.far, self.near, self.far2, self.near2 = far, near, far2, near2

    def axis(self, h, phase, d):
        return (d, 0) if h == phase else (0, d)

    def piece(self, h, f, s):
        a, b = self.axis(h, 0, f), self.axis(h, 1, s)
        return pl.ds(self.me.col_of(a[0] + b[0], a[1] + b[1]) * VB, VB)

    def start(self, source):
        me, wire = self.me, self.wire
        self.f_far, self.f_near = {}, {}
        for n, s in enumerate((2, 1, -1, 0)):
            for h in (0, 1):
                for w, d in ((0, 1), (1, -1)):
                    q = quarter(2 * h + w)
                    self.f_far[h, w, n] = wire.copy(
                        source.at[self.piece(h, 2, s), q, :], self.far.at[h, w, n], me.along_col(*self.axis(h, 0, d))
                    )
        for n, s in enumerate((2, 1, -1, 0)):
            for h in (0, 1):
                for w, d in ((0, 1), (1, -1)):
                    other = 1 - w
                    self.f_near[h, w, n, other] = wire.copy(
                        source.at[self.piece(h, d, s), quarter(2 * h + other), :],
                        self.near.at[h, w, n, other],
                        me.along_col(*self.axis(h, 0, d)),
                    )

    def rest(self):
        me, wire, part = self.me, self.wire, self.part
        for n, s in enumerate((2, 1, -1, 0)):
            for h in (0, 1):
                for w, d in ((0, 1), (1, -1)):
                    self.f_far[h, w, n].wait_recv()
                    at, q = self.piece(h, d, s), quarter(2 * h + w)
                    part[at, q, :] = (part[at, q, :].astype(f32) + self.far[h, w, n].astype(f32)).astype(bf16)
                    self.f_near[h, w, n, w] = wire.copy(
                        part.at[at, q, :], self.near.at[h, w, n, w], me.along_col(*self.axis(h, 0, d))
                    )
        s_far, s_near = {}, {}
        for n, s in enumerate((2, 1, -1, 0)):
            for h in (0, 1):
                at = self.piece(h, 0, s)
                for e in (0, 1):
                    for w in (0, 1):
                        self.f_near[h, w, n, e].wait_recv()
                    q = quarter(2 * h + e)
                    total = (
                        part[at, q, :].astype(f32)
                        + self.near[h, 0, n, e].astype(f32)
                        + self.near[h, 1, n, e].astype(f32)
                    )
                    d = 1 if e == 0 else -1
                    to = {1: me.along_col(*self.axis(h, 1, 1)), -1: me.along_col(*self.axis(h, 1, -1))}
                    if s == 2:
                        part[at, q, :] = total.astype(bf16)
                        s_far[h, e] = wire.copy(part.at[at, q, :], self.far2.at[h, e], to[d])
                    elif s == 0:
                        self.own_sum[:, q, :] = total
                    elif s == d:
                        s_far[h, e].wait_recv()
                        part[at, q, :] = (total + self.far2[h, e].astype(f32)).astype(bf16)
                        s_near[h, s, e] = wire.copy(part.at[at, q, :], self.near2.at[h, 0 if s == 1 else 1, e], to[s])
                    else:
                        part[at, q, :] = total.astype(bf16)
                        s_near[h, s, e] = wire.copy(part.at[at, q, :], self.near2.at[h, 0 if s == 1 else 1, e], to[s])
        for h in (0, 1):
            for e in (0, 1):
                s_near[h, 1, e].wait_recv()
                s_near[h, -1, e].wait_recv()
                self.own_sum[:, quarter(2 * h + e), :] += self.near2[h, 0, e].astype(f32) + self.near2[h, 1, e].astype(f32)


SUM_COPIES = 60


def step_kernel(
    ids, counts, grad, fetched, obs, own_store, new_store, arrived,
    part, own_sum, far, near, far2, near2, store_v, table, fetched_v, obs_v, terms, relay,
    sems, send_sem, recv_sem,
):
    me = Place()
    load_store = pltpu.make_async_copy(own_store, store_v, sems.at[0])
    load_part = pltpu.make_async_copy(grad, part, sems.at[1])
    load_store.start()
    load_part.start()
    peers = [me.along_row(*p) for p in PLACES[2:-1]]
    meet(col_peers(me) + peers)
    wire = Wire(send_sem, recv_sem)
    total = Sum(me, wire, part, own_sum, far, near, far2, near2)
    total.start(grad)
    load_part.wait()
    load_fetched = pltpu.make_async_copy(fetched, fetched_v, sems.at[2])
    load_fetched.start()
    load_obs = pltpu.make_async_copy(obs, obs_v, sems.at[3])
    load_obs.start()
    total.rest()
    load_store.wait()
    for v in range(VB):
        was = store_v[v]
        now = was - learn_rate * (own_sum[v].T + weight_decay * was)
        store_v[v] = now
        table[me.col * VB + v] = now.astype(bf16)
    gather = Gather(me, wire, None, table)
    keep_store = pltpu.make_async_copy(store_v, new_store, sems.at[4])
    keep_store.start()
    gather.middle()
    gather.end()
    load_fetched.wait()
    load_obs.wait()
    exchange = Exchange(me, wire, terms, arrived, relay)
    for j, p in enumerate(PLACES):
        o = me.row_of(*p)

        @pl.loop(0, CAP)
        def _(t):
            s = o * CAP + t
            x = fetched_v[o, t]
            now = obs_v.at[s]
            g = jnp.zeros((BS, R), f32)
            for k in range(0, K, 2):
                misfit, two = misfit_pair(x, table, ids[s, k], ids[s, k + 1], now, k)
                g = g + jnp.dot(misfit, two, preferred_element_type=f32)
            terms[j, t] = (g * (t < counts[o]).astype(f32)).astype(bf16)

        exchange.start(j)
        if j == 5:
            exchange.forward()
    keep_sku = pltpu.make_async_copy(terms.at[len(PLACES) - 1], arrived.at[me.row], sems.at[5])
    keep_sku.start()
    exchange.end()
    keep_sku.wait()
    keep_store.wait()
    wire.finish()


def last_step(requested, arrived, own, out, acc):
    acc[...] = jnp.zeros_like(acc)

    @pl.loop(0, SLOTS)
    def _(q):
        acc[requested[lax.div(q, CAP), 0, lax.rem(q, CAP)]] += arrived[q].astype(f32)

    out[...] = own[...] - learn_rate * (acc[...] + weight_decay * own[...])


SMEM = pl.BlockSpec(memory_space=pltpu.SMEM)
VMEM = pl.BlockSpec(memory_space=pltpu.VMEM)
ANY = pl.BlockSpec(memory_space=pl.ANY)
params = pltpu.CompilerParams(vmem_limit_bytes=VMEM_MOST)


def remote_params(n):
    return pltpu.CompilerParams(vmem_limit_bytes=VMEM_MOST, collective_id=n, has_side_effects=True)


def local(observed, sku_ids, store_ids, live_slot_counts, sku_factors, store_factors):
    counts = live_slot_counts.reshape(N_ROW)
    own_sku = sku_factors.reshape(UB, BS, R)
    own_store = store_factors.reshape(VB, BS, R)
    ids = jnp.pad(sku_ids.reshape(N_ROW, 1, CAP), ((0, 0), (0, 7), (0, 124)))
    group_low, fetched, requested = pl.pallas_call(
        gather_kernel,
        out_shape=(
            jax.ShapeDtypeStruct((VG, BS, R), bf16),
            jax.ShapeDtypeStruct((N_ROW, CAP, BS, R), bf16),
            jax.ShapeDtypeStruct((N_ROW, 8, 128), jnp.int32),
        ),
        in_specs=[VMEM, ANY, ANY],
        out_specs=(ANY, ANY, ANY),
        scratch_shapes=[
            pltpu.VMEM((UB, BS, R), f32),
            pltpu.VMEM((VB, BS, R), f32),
            pltpu.VMEM((VB, BS, R), bf16),
            pltpu.VMEM((N_ROW, CAP, BS, R), bf16),
            pltpu.VMEM((2, 2, 2, BS, R), bf16),
            pltpu.VMEM((N_ROW, 8, 128), jnp.int32),
            pltpu.SMEM((N_ROW, 8, 128), jnp.int32),
            pltpu.SemaphoreType.DMA((7,)),
            pltpu.SemaphoreType.DMA((7 + GATHER_COPIES + EXCHANGE_COPIES,)),
            pltpu.SemaphoreType.DMA((7 + GATHER_COPIES + EXCHANGE_COPIES,)),
        ],
        compiler_params=remote_params(0),
        name="gather_kernel",
    )(ids, own_sku, own_store)
    grad = pl.pallas_call(
        first_pass,
        out_shape=jax.ShapeDtypeStruct((VG, R, BS), bf16),
        in_specs=[SMEM, SMEM, ANY, ANY, VMEM],
        out_specs=VMEM,
        scratch_shapes=[
            pltpu.VMEM((VG, R, BS), f32),
            pltpu.SMEM((SLOTS + 1,), jnp.int32),
            pltpu.VMEM((DEPTH, BS, R), bf16),
            pltpu.VMEM((DEPTH, K, BS, BS), bf16),
            pltpu.SemaphoreType.DMA((2, DEPTH)),
        ],
        compiler_params=params,
        name="first_pass",
    )(store_ids, counts, fetched, observed, group_low)
    new_store, arrived = pl.pallas_call(
        step_kernel,
        out_shape=(
            jax.ShapeDtypeStruct((VB, BS, R), f32),
            jax.ShapeDtypeStruct((N_ROW, CAP, BS, R), bf16),
        ),
        in_specs=[SMEM, SMEM, ANY, ANY, ANY, ANY],
        out_specs=(ANY, ANY),
        scratch_shapes=[
            pltpu.VMEM((VG, R, BS), bf16),
            pltpu.VMEM((VB, R, BS), f32),
            pltpu.VMEM((2, 2, RING, VB, R // 4, BS), bf16),
            pltpu.VMEM((2, 2, RING, 2, VB, R // 4, BS), bf16),
            pltpu.VMEM((2, 2, VB, R // 4, BS), bf16),
            pltpu.VMEM((2, 2, 2, VB, R // 4, BS), bf16),
            pltpu.VMEM((VB, BS, R), f32),
            pltpu.VMEM((VG, BS, R), bf16),
            pltpu.VMEM((N_ROW, CAP, BS, R), bf16),
            pltpu.VMEM((SLOTS, K, BS, BS), bf16),
            pltpu.VMEM((N_ROW, CAP, BS, R), bf16),
            pltpu.VMEM((2, 2, 2, BS, R), bf16),
            pltpu.SemaphoreType.DMA((6,)),
            pltpu.SemaphoreType.DMA((SUM_COPIES + GATHER_COPIES + EXCHANGE_COPIES,)),
            pltpu.SemaphoreType.DMA((SUM_COPIES + GATHER_COPIES + EXCHANGE_COPIES,)),
        ],
        compiler_params=remote_params(1),
        name="step_kernel",
    )(store_ids, counts, grad, fetched, observed, own_store)
    new_sku = pl.pallas_call(
        last_step,
        out_shape=jax.ShapeDtypeStruct((UB, BS, R), f32),
        in_specs=[SMEM, VMEM, VMEM],
        out_specs=VMEM,
        scratch_shapes=[pltpu.VMEM((UB, BS, R), f32)],
        compiler_params=params,
        name="last_step",
    )(requested, arrived.reshape(SLOTS, BS, R), own_sku)
    return new_sku.reshape(sku_factors.shape), new_store.reshape(store_factors.shape)


def solution(mesh):
    placed = (
        P(("row", "col"), None, None, None),
        P(("row", "col")),
        P(("row", "col"), None),
        P("row", "col", None),
        P(("row", "col"), None),
        P(("row", "col"), None),
    )
    return jax.shard_map(
        local,
        mesh=mesh,
        in_specs=placed,
        out_specs=(P(("row", "col"), None), P(("row", "col"), None)),
        check_vma=False,
    )
```

time: 353 us -> 163 us (0.46)
  waiting for transfers between devices: 269 us -> 0 us
  Pallas kernels: 36.5 us -> 158 us
  between operations: 13.8 us -> 0.66 us
  starting transfers between devices: 10.8 us -> 0 us
  local copies, waits for them, and re-layouts: 11.6 us -> 3.56 us
  other arithmetic: 7.21 us -> 0 us
    all_gather x3 -> x0, waiting for transfers between devices: 161 us -> none  [the longest x1 57.9 us: local(): lax.all_gather(own_store.astype(bf16), 'col', axis=0, tiled=True)]
    pallas_call x1 -> x2, Pallas kernels: 13.1 us -> 131 us  [the longest x1 93.7 us: local(): pl.pallas_call(step_kernel, out_shape=(jax.ShapeDtypeStruct((VB, BS, R),...]
    unnamed x5 -> x0, waiting for transfers between devices: 84.1 us -> none
    all_to_all x2 -> x0, waiting for transfers between devices: 24.5 us -> none  [the longest x1 24.5 us: local(): lax.all_to_all(terms.reshape(N_ROW, CAP, BS, R), 'row', split_axis=0, con...]
    all_to_all x2 -> x0, starting transfers between devices: 10.6 us -> none  [the longest x1 5.98 us: local(): lax.all_to_all(sku_ids.reshape(N_ROW, CAP), 'row', split_axis=0, concat_a...]
    pallas_call x1 -> x0, local copies, waits for them, and re-layouts: 7.77 us -> none  [local(): pl.pallas_call(first_pass, out_shape=jax.ShapeDtypeStruct((VG, R, BS), bf...]
    convert_element_type x3 -> x0, other arithmetic: 6.57 us -> none  [the longest x1 2.69 us: local(): tables = lax.all_gather(own_sku.astype(bf16), 'row', axis=0, tiled=True)]
  transfers between devices with their start and end apart: 6 -> 0, of which waited for: 5 -> 0; matrix products, arithmetic and copies ran while one was open for 1% -> 0% of each run, Pallas kernels for 4% -> 0%
where the time goes in v2:
time: 163 us; the launch traced here: 162 us
  Pallas kernels  158 us (97%)
  local copies, waits for them, and re-layouts  3.56 us (2%)
    pallas_call x1, Pallas kernels, local(): pl.pallas_call(step_kernel, out_shape=(jax.ShapeDtypeStruct((VB, BS, R),...  93.7 us
    pallas_call x1, Pallas kernels, local(): pl.pallas_call(gather_kernel, out_shape=(jax.ShapeDtypeStruct((VG, BS, R)...  37.6 us
    pallas_call x1, Pallas kernels, local(): pl.pallas_call(first_pass, out_shape=jax.ShapeDtypeStruct((VG, R, BS), bf...  22 us
    pallas_call x1, Pallas kernels, local(): pl.pallas_call(last_step, out_shape=jax.ShapeDtypeStruct((UB, BS, R), f32...  4.69 us

profile of v2, /device:TPU:1, one launch (start us, length us, event | category | flops | bytes accessed | tf_op | source)
XLA Modules:
  0.0 162.3 jit_solution(3501674383779345833)
XLA Ops:
  0.6 0.7 reshape.25
  1.4 1.4 copy.13.ids
  2.7 0.6 pad.4.ids
  3.4 37.6 %gather_kernel.1 = (bf16[80,128,256]{2,1,0:T(8,128)(2,1)}, bf16[8,4,128,256]{3,2,1,0:T(8,128)(2,1)}, s32[8,8,128]{2,1,0:T(8,128)}) custom-call(s32[8,8,128]{2,1,0:T(8,128)} %pad.4.ids, f32[16,128,256]{2,1,0:T(8,128)} %bitcast.7, f32[5,128,256]{2,1,0:T(8,128)} %bitcast.9), custom_call_target="tpu_custom_call" | custom-call | tf_op jit(solution)/shard_map/gather_kernel/pallas_call | solution.py:458
  41.0 22.0 %first_pass.1.grad = bf16[80,256,128]{2,1,0:T(8,128)(2,1)} custom-call(s32[32,8]{1,0:T(8,128)} %copy.13.ids, s32[8]{0:T(128)} %bitcast.15, bf16[8,4,128,256]{3,2,1,0:T(8,128)(2,1)} %get-tuple-element.8.fetched, bf16[32,8,128,128]{3,2,1,0:T(8,128)(2,1)} %obs.3, bf16[80,128,256]{2,1,0:T(8,128)(2,1)} %get-tuple-element.9.store), custom_call_target="tpu_custom_call" | custom-call | tf_op jit(solution)/shard_map/first_pass/pallas_call | solution.py:482
  63.0 93.7 %step_kernel.1 = (f32[5,128,256]{2,1,0:T(8,128)}, bf16[8,4,128,256]{3,2,1,0:T(8,128)(2,1)}) custom-call(s32[32,8]{1,0:T(8,128)} %copy.13.ids, s32[8]{0:T(128)} %bitcast.16, bf16[80,256,128]{2,1,0:T(8,128)(2,1)} %first_pass.1.grad, bf16[8,4,128,256]{3,2,1,0:T(8,128)(2,1)} %get-tuple-element.8.fetched, bf16[32,8,128,128]{3,2,1,0:T(8,128)(2,1)} %obs.3, ...), custom_call_target="tpu_custom_call" | custom-call | tf_op jit(solution)/shard_map/step_kernel/pallas_call | solution.py:497
  156.7 0.0 copy-start
  156.7 4.7 %last_step.1 = f32[16,128,256]{2,1,0:T(8,128)} custom-call(s32[8,8,128]{2,1,0:T(8,128)} %get-tuple-element.7.requested, bf16[32,128,256]{2,1,0:T(8,128)(2,1)} %bitcast.12, f32[16,128,256]{2,1,0:T(8,128)} %bitcast.8), custom_call_target="tpu_custom_call" | custom-call | tf_op jit(solution)/shard_map/last_step/pallas_call | solution.py:525
  161.4 0.0 copy-done
  161.4 0.8 copy.15
Async XLA Ops:
  156.7 4.7 %copy-start = (f32[5,128,256]{2,1,0:T(8,128)S(1)}, f32[5,128,256]{2,1,0:T(8,128)}, u32[]{:S(2)}) copy-start(f32[5,128,256]{2,1,0:T(8,128)} %get-tuple-element.11) | copy-start | bytes 1966084

commit v3 on v2

--- a/solution.py
+++ b/solution.py
@@ -17,6 +17,7 @@
 VB = 5
 VG = 80
 DEPTH = 4
+CHUNKS = 8
 VMEM_MOST = 60 * 1024 * 1024
 
 RING = 4
@@ -42,7 +43,12 @@
     return (predicted - measured.astype(f32)).astype(bf16), two
 
 
-def first_pass(ids, counts, fetched, obs, store, out, acc, order, sku_buf, obs_buf, sem):
+def first_pass(
+    ids, counts, fetched, obs, group, out,
+    store, acc, order, sku_buf, obs_buf, misfits, staged, sem, end_sem,
+):
+    load_store = pltpu.make_async_copy(group, store, end_sem.at[CHUNKS])
+    load_store.start()
     total = live_list(counts, order)
 
     def copies(i):
@@ -53,6 +59,11 @@
             pltpu.make_async_copy(obs.at[s], obs_buf.at[at], sem.at[1, at]),
         )
 
+    def misfit(i, k):
+        s = order[i]
+        at = lax.rem(i, DEPTH)
+        return misfit_pair(sku_buf[at], store, ids[k, s], ids[k + 1, s], obs_buf.at[at], k)[0]
+
     for i in range(DEPTH - 1):
 
         @pl.when(i < total)
@@ -61,6 +72,14 @@
                 c.start()
 
     acc[...] = jnp.zeros_like(acc)
+    load_store.wait()
+
+    @pl.when(total > 0)
+    def _():
+        for c in copies(0):
+            c.wait()
+        for k in range(0, K, 2):
+            misfits[k // 2] = misfit(0, k)
 
     @pl.loop(0, total)
     def _(i):
@@ -69,21 +88,31 @@
             for c in copies(i + DEPTH - 1):
                 c.start()
 
-        for c in copies(i):
-            c.wait()
+        @pl.when(i + 1 < total)
+        def _():
+            for c in copies(i + 1):
+                c.wait()
+
         s = order[i]
-        at = lax.rem(i, DEPTH)
-        x = sku_buf[at]
-        xt = x.T
-        now = obs_buf.at[at]
+        later = jnp.minimum(i + 1, total - 1)
+        xt = sku_buf[lax.rem(i, DEPTH)].T
         for k in range(0, K, 2):
-            a, b = ids[s, k], ids[s, k + 1]
-            misfit, _ = misfit_pair(x, store, a, b, now, k)
-            g = jnp.dot(xt, misfit, preferred_element_type=f32)
+            a, b = ids[k, s], ids[k + 1, s]
+            g = jnp.dot(xt, misfits[k // 2], preferred_element_type=f32)
+            misfits[k // 2] = misfit(later, k)
             acc[a] += g[:, :BS]
             acc[b] += g[:, BS:]
 
-    out[...] = acc[...].astype(bf16)
+    n = VG // CHUNKS
+    stores = []
+    for q in range(CHUNKS):
+        part = pl.ds(q * n, n)
+        staged[part] = acc[part].astype(bf16)
+        c = pltpu.make_async_copy(staged.at[part], out.at[part], end_sem.at[q])
+        c.start()
+        stores.append(c)
+    for c in stores:
+        c.wait()
 
 
 class Place:
@@ -240,20 +269,22 @@
 
 def gather_kernel(
     ids, own_sku, own_store, group, fetched, requests,
-    sku_v, store_v, low, send, relay, heard, heard_s, sems, send_sem, recv_sem,
+    ids_v, sku_v, store_v, low, send, relay, heard, heard_s, sems, send_sem, recv_sem,
 ):
     me = Place()
     load_store = pltpu.make_async_copy(own_store, store_v, sems.at[0])
     load_sku = pltpu.make_async_copy(own_sku, sku_v, sems.at[1])
     load_store.start()
     load_sku.start()
+    ids_v[...] = jnp.zeros_like(ids_v)
+    ids_v[0:1, 0:SLOTS] = ids[...]
     peers = [me.along_row(*p) for p in PLACES[:-1]]
     meet(col_peers(me) + peers)
     wire = Wire(send_sem, recv_sem)
     asked = [
-        wire.copy(ids.at[me.row_of(*p)], heard.at[me.row], me.along_row(*p)) for p in PLACES[:-1]
+        wire.copy(ids_v, heard.at[me.row], me.along_row(*p)) for p in PLACES[:-1]
     ]
-    own_ids = pltpu.make_async_copy(ids.at[me.row], heard.at[me.row], sems.at[2])
+    own_ids = pltpu.make_async_copy(ids_v, heard.at[me.row], sems.at[2])
     own_ids.start()
     load_store.wait()
     low[...] = store_v[...].astype(bf16)
@@ -272,7 +303,7 @@
     exchange = Exchange(me, wire, send, fetched, relay)
     for j, p in enumerate(PLACES):
         for t in range(CAP):
-            send[j, t] = sku_v[heard_s[me.row_of(*p), 0, t]].astype(bf16)
+            send[j, t] = sku_v[heard_s[me.row_of(*p), 0, me.row * CAP + t]].astype(bf16)
         exchange.start(j)
     keep_sku = pltpu.make_async_copy(send.at[len(PLACES) - 1], fetched.at[me.row], sems.at[6])
     keep_sku.start()
@@ -415,7 +446,7 @@
             now = obs_v.at[s]
             g = jnp.zeros((BS, R), f32)
             for k in range(0, K, 2):
-                misfit, two = misfit_pair(x, table, ids[s, k], ids[s, k + 1], now, k)
+                misfit, two = misfit_pair(x, table, ids[k, s], ids[k + 1, s], now, k)
                 g = g + jnp.dot(misfit, two, preferred_element_type=f32)
             terms[j, t] = (g * (t < counts[o]).astype(f32)).astype(bf16)
 
@@ -430,14 +461,15 @@
     wire.finish()
 
 
-def last_step(requested, arrived, own, out, acc):
-    acc[...] = jnp.zeros_like(acc)
-
-    @pl.loop(0, SLOTS)
-    def _(q):
-        acc[requested[lax.div(q, CAP), 0, lax.rem(q, CAP)]] += arrived[q].astype(f32)
-
-    out[...] = own[...] - learn_rate * (acc[...] + weight_decay * own[...])
+def last_step(requested, arrived, own, store, out, new_store):
+    new_store[...] = store[...]
+    row = lax.axis_index("row")
+    out[...] = own[...] * (1 - learn_rate * weight_decay)
+
+    @pl.loop(0, N_ROW)
+    def _(o):
+        for t in range(CAP):
+            out[requested[o, 0, row * CAP + t]] -= learn_rate * arrived[o * CAP + t].astype(f32)
 
 
 SMEM = pl.BlockSpec(memory_space=pltpu.SMEM)
@@ -454,7 +486,7 @@
     counts = live_slot_counts.reshape(N_ROW)
     own_sku = sku_factors.reshape(UB, BS, R)
     own_store = store_factors.reshape(VB, BS, R)
-    ids = jnp.pad(sku_ids.reshape(N_ROW, 1, CAP), ((0, 0), (0, 7), (0, 124)))
+    store_ids = store_ids.T
     group_low, fetched, requested = pl.pallas_call(
         gather_kernel,
         out_shape=(
@@ -465,6 +497,7 @@
         in_specs=[VMEM, ANY, ANY],
         out_specs=(ANY, ANY, ANY),
         scratch_shapes=[
+            pltpu.VMEM((8, 128), jnp.int32),
             pltpu.VMEM((UB, BS, R), f32),
             pltpu.VMEM((VB, BS, R), f32),
             pltpu.VMEM((VB, BS, R), bf16),
@@ -478,18 +511,22 @@
         ],
         compiler_params=remote_params(0),
         name="gather_kernel",
-    )(ids, own_sku, own_store)
+    )(sku_ids.reshape(1, SLOTS), own_sku, own_store)
     grad = pl.pallas_call(
         first_pass,
         out_shape=jax.ShapeDtypeStruct((VG, R, BS), bf16),
-        in_specs=[SMEM, SMEM, ANY, ANY, VMEM],
-        out_specs=VMEM,
+        in_specs=[SMEM, SMEM, ANY, ANY, ANY],
+        out_specs=ANY,
         scratch_shapes=[
+            pltpu.VMEM((VG, BS, R), bf16),
             pltpu.VMEM((VG, R, BS), f32),
             pltpu.SMEM((SLOTS + 1,), jnp.int32),
             pltpu.VMEM((DEPTH, BS, R), bf16),
             pltpu.VMEM((DEPTH, K, BS, BS), bf16),
+            pltpu.VMEM((K // 2, BS, 2 * BS), bf16),
+            pltpu.VMEM((VG, R, BS), bf16),
             pltpu.SemaphoreType.DMA((2, DEPTH)),
+            pltpu.SemaphoreType.DMA((CHUNKS + 1,)),
         ],
         compiler_params=params,
         name="first_pass",
@@ -522,15 +559,19 @@
         compiler_params=remote_params(1),
         name="step_kernel",
     )(store_ids, counts, grad, fetched, observed, own_store)
-    new_sku = pl.pallas_call(
+    part = lambda n: pl.BlockSpec((n, BS // 2, R), lambda i: (0, i, 0))
+    new_sku, new_store = pl.pallas_call(
         last_step,
-        out_shape=jax.ShapeDtypeStruct((UB, BS, R), f32),
-        in_specs=[SMEM, VMEM, VMEM],
-        out_specs=VMEM,
-        scratch_shapes=[pltpu.VMEM((UB, BS, R), f32)],
+        out_shape=(
+            jax.ShapeDtypeStruct((UB, BS, R), f32),
+            jax.ShapeDtypeStruct((VB, BS, R), f32),
+        ),
+        grid=(2,),
+        in_specs=[SMEM, part(SLOTS), part(UB), part(VB)],
+        out_specs=(part(UB), part(VB)),
         compiler_params=params,
         name="last_step",
-    )(requested, arrived.reshape(SLOTS, BS, R), own_sku)
+    )(requested, arrived.reshape(SLOTS, BS, R), own_sku, new_store)
     return new_sku.reshape(sku_factors.shape), new_store.reshape(store_factors.shape)
 
 

time: 163 us -> 152 us (0.933)
  Pallas kernels: 158 us -> 151 us
  local copies, waits for them, and re-layouts: 3.56 us -> 0 us
    pallas_call x1, Pallas kernels: 22 us -> 15.3 us  [local(): pl.pallas_call(first_pass, out_shape=jax.ShapeDtypeStruct((VG, R, BS), bf...]
    unnamed x4 -> x0, local copies, waits for them, and re-layouts: 2.21 us -> none
where the time goes in v3:
time: 152 us
  Pallas kernels  151 us (99%)
    pallas_call x1, Pallas kernels, local(): pl.pallas_call(step_kernel, out_shape=(jax.ShapeDtypeStruct((VB, BS, R),...  94.4 us
    pallas_call x1, Pallas kernels, local(): pl.pallas_call(gather_kernel, out_shape=(jax.ShapeDtypeStruct((VG, BS, R)...  37.6 us
    pallas_call x1, Pallas kernels, local(): pl.pallas_call(first_pass, out_shape=jax.ShapeDtypeStruct((VG, R, BS), bf...  15.3 us
    pallas_call x1, Pallas kernels, local(): pl.pallas_call(last_step, out_shape=(jax.ShapeDtypeStruct((UB, BS, R), f3...  3.87 us

profile of v3, /device:TPU:1, one launch (start us, length us, event | category | flops | bytes accessed | tf_op | source)
XLA Modules:
  0.0 151.8 jit_solution(12557246020907327105)
XLA Ops:
  0.6 37.6 %gather_kernel.1 = (bf16[80,128,256]{2,1,0:T(8,128)(2,1)}, bf16[8,4,128,256]{3,2,1,0:T(8,128)(2,1)}, s32[8,8,128]{2,1,0:T(8,128)}) custom-call(s32[1,32]{1,0:T(1,128)} %bitcast.17, f32[16,128,256]{2,1,0:T(8,128)} %bitcast.8, f32[5,128,256]{2,1,0:T(8,128)} %bitcast.10), custom_call_target="tpu_custom_call" | custom-call | tf_op jit(solution)/shard_map/gather_kernel/pallas_call | solution.py:490
  38.2 15.3 %first_pass.1.grad = bf16[80,256,128]{2,1,0:T(8,128)(2,1)} custom-call(s32[8,32]{1,0:T(8,128)} %bitcast.13, s32[8]{0:T(128)} %bitcast.15, bf16[8,4,128,256]{3,2,1,0:T(8,128)(2,1)} %get-tuple-element.10.fetched, bf16[32,8,128,128]{3,2,1,0:T(8,128)(2,1)} %obs.3, bf16[80,128,256]{2,1,0:T(8,128)(2,1)} %get-tuple-element.11.group), custom_call_target="tpu_custom_call" | custom-call | tf_op jit(solution)/shard_map/first_pass/pallas_call | solution.py:515
  53.5 94.4 %step_kernel.1 = (f32[5,128,256]{2,1,0:T(8,128)}, bf16[8,4,128,256]{3,2,1,0:T(8,128)(2,1)}) custom-call(s32[8,32]{1,0:T(8,128)} %bitcast.14, s32[8]{0:T(128)} %bitcast.16, bf16[80,256,128]{2,1,0:T(8,128)(2,1)} %first_pass.1.grad, bf16[8,4,128,256]{3,2,1,0:T(8,128)(2,1)} %get-tuple-element.10.fetched, bf16[32,8,128,128]{3,2,1,0:T(8,128)(2,1)} %obs.3, ...), custom_call_target="tpu_custom_call" | custom-call | tf_op jit(solution)/shard_map/step_kernel/pallas_call | solution.py:534
  147.9 3.9 %last_step.1 = (f32[16,128,256]{2,1,0:T(8,128)}, f32[5,128,256]{2,1,0:T(8,128)}) custom-call(s32[8,8,128]{2,1,0:T(8,128)} %get-tuple-element.9.requested, bf16[32,128,256]{2,1,0:T(8,128)(2,1)} %bitcast.12, f32[16,128,256]{2,1,0:T(8,128)} %bitcast.9, f32[5,128,256]{2,1,0:T(8,128)} %get-tuple-element.13.store), custom_call_target="tpu_custom_call" | custom-call | tf_op jit(solution)/shard_map/last_step/pallas_call | solution.py:563

commit v4 on v3

--- a/solution.py
+++ b/solution.py
@@ -36,11 +36,10 @@
     return total
 
 
-def misfit_pair(x, store, first, second, obs, k):
-    two = jnp.concatenate([store[first], store[second]], axis=0)
+def misfit_pair(x, two, obs, k):
     predicted = lax.dot_general(x, two, NT, preferred_element_type=f32)
     measured = jnp.concatenate([obs[k], obs[k + 1]], axis=1)
-    return (predicted - measured.astype(f32)).astype(bf16), two
+    return (predicted - measured.astype(f32)).astype(bf16)
 
 
 def first_pass(
@@ -62,7 +61,8 @@
     def misfit(i, k):
         s = order[i]
         at = lax.rem(i, DEPTH)
-        return misfit_pair(sku_buf[at], store, ids[k, s], ids[k + 1, s], obs_buf.at[at], k)[0]
+        two = jnp.concatenate([store[ids[k, s]], store[ids[k + 1, s]]], axis=0)
+        return misfit_pair(sku_buf[at], two, obs_buf.at[at], k)
 
     for i in range(DEPTH - 1):
 
@@ -317,17 +317,21 @@
     wire.finish()
 
 
-def quarter(q):
-    return pl.ds(q * (R // 4), R // 4)
+STREAMS = 2
+WIDTH = R // STREAMS
+PART = WIDTH // 4
 
 
 class Sum:
-    def __init__(self, me, wire, part, own_sum, far, near, far2, near2):
-        self.me, self.wire, self.part, self.own_sum = me, wire, part, own_sum
+    def __init__(self, me, wire, stream, part, own_sum, far, near, far2, near2):
+        self.me, self.wire, self.stream, self.part, self.own_sum = me, wire, stream, part, own_sum
         self.far, self.near, self.far2, self.near2 = far, near, far2, near2
 
     def axis(self, h, phase, d):
         return (d, 0) if h == phase else (0, d)
+
+    def quarter(self, q):
+        return pl.ds(self.stream * WIDTH + q * PART, PART)
 
     def piece(self, h, f, s):
         a, b = self.axis(h, 0, f), self.axis(h, 1, s)
@@ -339,7 +343,7 @@
         for n, s in enumerate((2, 1, -1, 0)):
             for h in (0, 1):
                 for w, d in ((0, 1), (1, -1)):
-                    q = quarter(2 * h + w)
+                    q = self.quarter(2 * h + w)
                     self.f_far[h, w, n] = wire.copy(
                         source.at[self.piece(h, 2, s), q, :], self.far.at[h, w, n], me.along_col(*self.axis(h, 0, d))
                     )
@@ -348,22 +352,25 @@
                 for w, d in ((0, 1), (1, -1)):
                     other = 1 - w
                     self.f_near[h, w, n, other] = wire.copy(
-                        source.at[self.piece(h, d, s), quarter(2 * h + other), :],
+                        source.at[self.piece(h, d, s), self.quarter(2 * h + other), :],
                         self.near.at[h, w, n, other],
                         me.along_col(*self.axis(h, 0, d)),
                     )
 
-    def rest(self):
+    def near_sums(self):
         me, wire, part = self.me, self.wire, self.part
         for n, s in enumerate((2, 1, -1, 0)):
             for h in (0, 1):
                 for w, d in ((0, 1), (1, -1)):
                     self.f_far[h, w, n].wait_recv()
-                    at, q = self.piece(h, d, s), quarter(2 * h + w)
+                    at, q = self.piece(h, d, s), self.quarter(2 * h + w)
                     part[at, q, :] = (part[at, q, :].astype(f32) + self.far[h, w, n].astype(f32)).astype(bf16)
                     self.f_near[h, w, n, w] = wire.copy(
                         part.at[at, q, :], self.near.at[h, w, n, w], me.along_col(*self.axis(h, 0, d))
                     )
+
+    def rest(self):
+        me, wire, part = self.me, self.wire, self.part
         s_far, s_near = {}, {}
         for n, s in enumerate((2, 1, -1, 0)):
             for h in (0, 1):
@@ -371,7 +378,7 @@
                 for e in (0, 1):
                     for w in (0, 1):
                         self.f_near[h, w, n, e].wait_recv()
-                    q = quarter(2 * h + e)
+                    q = self.quarter(2 * h + e)
                     total = (
                         part[at, q, :].astype(f32)
                         + self.near[h, 0, n, e].astype(f32)
@@ -395,7 +402,7 @@
             for e in (0, 1):
                 s_near[h, 1, e].wait_recv()
                 s_near[h, -1, e].wait_recv()
-                self.own_sum[:, quarter(2 * h + e), :] += self.near2[h, 0, e].astype(f32) + self.near2[h, 1, e].astype(f32)
+                self.own_sum[:, self.quarter(2 * h + e), :] += self.near2[h, 0, e].astype(f32) + self.near2[h, 1, e].astype(f32)
 
 
 SUM_COPIES = 60
@@ -414,28 +421,44 @@
     peers = [me.along_row(*p) for p in PLACES[2:-1]]
     meet(col_peers(me) + peers)
     wire = Wire(send_sem, recv_sem)
-    total = Sum(me, wire, part, own_sum, far, near, far2, near2)
-    total.start(grad)
+    sums = [
+        Sum(me, wire, c, part, own_sum, far.at[c], near.at[c], far2.at[c], near2.at[c]) for c in range(STREAMS)
+    ]
+    sums[0].start(grad)
     load_part.wait()
     load_fetched = pltpu.make_async_copy(fetched, fetched_v, sems.at[2])
     load_fetched.start()
     load_obs = pltpu.make_async_copy(obs, obs_v, sems.at[3])
     load_obs.start()
-    total.rest()
     load_store.wait()
-    for v in range(VB):
-        was = store_v[v]
-        now = was - learn_rate * (own_sum[v].T + weight_decay * was)
-        store_v[v] = now
-        table[me.col * VB + v] = now.astype(bf16)
-    gather = Gather(me, wire, None, table)
+    sums[0].near_sums()
+    gathers = []
+    for c in range(STREAMS):
+        if c + 1 < STREAMS:
+            sums[c + 1].start(grad)
+        else:
+            sums[c].near_sums()
+        sums[c].rest()
+        lanes = pl.ds(c * WIDTH, WIDTH)
+        for v in range(VB):
+            was = store_v[v, :, lanes]
+            now = was - learn_rate * (own_sum[v, lanes, :].T + weight_decay * was)
+            store_v[v, :, lanes] = now
+            table[c, me.col * VB + v] = now.astype(bf16)
+        gathers.append(Gather(me, wire, None, table.at[c]))
     keep_store = pltpu.make_async_copy(store_v, new_store, sems.at[4])
     keep_store.start()
-    gather.middle()
-    gather.end()
+    for g in gathers:
+        g.middle()
+    for g in gathers:
+        g.end()
     load_fetched.wait()
     load_obs.wait()
     exchange = Exchange(me, wire, terms, arrived, relay)
+
+    def block(i):
+        return jnp.concatenate([table[c, i] for c in range(STREAMS)], axis=1)
+
     for j, p in enumerate(PLACES):
         o = me.row_of(*p)
 
@@ -446,7 +469,8 @@
             now = obs_v.at[s]
             g = jnp.zeros((BS, R), f32)
             for k in range(0, K, 2):
-                misfit, two = misfit_pair(x, table, ids[k, s], ids[k + 1, s], now, k)
+                two = jnp.concatenate([block(ids[k, s]), block(ids[k + 1, s])], axis=0)
+                misfit = misfit_pair(x, two, now, k)
                 g = g + jnp.dot(misfit, two, preferred_element_type=f32)
             terms[j, t] = (g * (t < counts[o]).astype(f32)).astype(bf16)
 
@@ -542,19 +566,19 @@
         scratch_shapes=[
             pltpu.VMEM((VG, R, BS), bf16),
             pltpu.VMEM((VB, R, BS), f32),
-            pltpu.VMEM((2, 2, RING, VB, R // 4, BS), bf16),
-            pltpu.VMEM((2, 2, RING, 2, VB, R // 4, BS), bf16),
-            pltpu.VMEM((2, 2, VB, R // 4, BS), bf16),
-            pltpu.VMEM((2, 2, 2, VB, R // 4, BS), bf16),
+            pltpu.VMEM((STREAMS, 2, 2, RING, VB, PART, BS), bf16),
+            pltpu.VMEM((STREAMS, 2, 2, RING, 2, VB, PART, BS), bf16),
+            pltpu.VMEM((STREAMS, 2, 2, VB, PART, BS), bf16),
+            pltpu.VMEM((STREAMS, 2, 2, 2, VB, PART, BS), bf16),
             pltpu.VMEM((VB, BS, R), f32),
-            pltpu.VMEM((VG, BS, R), bf16),
+            pltpu.VMEM((STREAMS, VG, BS, WIDTH), bf16),
             pltpu.VMEM((N_ROW, CAP, BS, R), bf16),
             pltpu.VMEM((SLOTS, K, BS, BS), bf16),
             pltpu.VMEM((N_ROW, CAP, BS, R), bf16),
             pltpu.VMEM((2, 2, 2, BS, R), bf16),
             pltpu.SemaphoreType.DMA((6,)),
-            pltpu.SemaphoreType.DMA((SUM_COPIES + GATHER_COPIES + EXCHANGE_COPIES,)),
-            pltpu.SemaphoreType.DMA((SUM_COPIES + GATHER_COPIES + EXCHANGE_COPIES,)),
+            pltpu.SemaphoreType.DMA((STREAMS * (SUM_COPIES + GATHER_COPIES) + EXCHANGE_COPIES,)),
+            pltpu.SemaphoreType.DMA((STREAMS * (SUM_COPIES + GATHER_COPIES) + EXCHANGE_COPIES,)),
         ],
         compiler_params=remote_params(1),
         name="step_kernel",

time: 152 us -> 163 us (1.072)
  Pallas kernels: 151 us -> 162 us
    pallas_call x1, Pallas kernels: 94.4 us -> 106 us  [local(): pl.pallas_call(step_kernel, out_shape=(jax.ShapeDtypeStruct((VB, BS, R),...]
where the time goes in v4:
time: 163 us
  Pallas kernels  162 us (99%)
    pallas_call x1, Pallas kernels, local(): pl.pallas_call(step_kernel, out_shape=(jax.ShapeDtypeStruct((VB, BS, R),...  106 us
    pallas_call x1, Pallas kernels, local(): pl.pallas_call(gather_kernel, out_shape=(jax.ShapeDtypeStruct((VG, BS, R)...  37.6 us
    pallas_call x1, Pallas kernels, local(): pl.pallas_call(first_pass, out_shape=jax.ShapeDtypeStruct((VG, R, BS), bf...  14.3 us
    pallas_call x1, Pallas kernels, local(): pl.pallas_call(last_step, out_shape=(jax.ShapeDtypeStruct((UB, BS, R), f3...  3.87 us

profile of v4, /device:TPU:1, one launch (start us, length us, event | category | flops | bytes accessed | tf_op | source)
XLA Modules:
  0.0 162.6 jit_solution(7010106816700286681)
XLA Ops:
  0.6 37.6 %gather_kernel.1 = (bf16[80,128,256]{2,1,0:T(8,128)(2,1)}, bf16[8,4,128,256]{3,2,1,0:T(8,128)(2,1)}, s32[8,8,128]{2,1,0:T(8,128)}) custom-call(s32[1,32]{1,0:T(1,128)} %bitcast.17, f32[16,128,256]{2,1,0:T(8,128)} %bitcast.8, f32[5,128,256]{2,1,0:T(8,128)} %bitcast.10), custom_call_target="tpu_custom_call" | custom-call | tf_op jit(solution)/shard_map/gather_kernel/pallas_call | solution.py:514
  38.2 14.3 %first_pass.1.grad = bf16[80,256,128]{2,1,0:T(8,128)(2,1)} custom-call(s32[8,32]{1,0:T(8,128)} %bitcast.13, s32[8]{0:T(128)} %bitcast.15, bf16[8,4,128,256]{3,2,1,0:T(8,128)(2,1)} %get-tuple-element.10.fetched, bf16[32,8,128,128]{3,2,1,0:T(8,128)(2,1)} %obs.3, bf16[80,128,256]{2,1,0:T(8,128)(2,1)} %get-tuple-element.11.group), custom_call_target="tpu_custom_call" | custom-call | tf_op jit(solution)/shard_map/first_pass/pallas_call | solution.py:539
  52.5 106.2 %step_kernel.1 = (f32[5,128,256]{2,1,0:T(8,128)}, bf16[8,4,128,256]{3,2,1,0:T(8,128)(2,1)}) custom-call(s32[8,32]{1,0:T(8,128)} %bitcast.14, s32[8]{0:T(128)} %bitcast.16, bf16[80,256,128]{2,1,0:T(8,128)(2,1)} %first_pass.1.grad, bf16[8,4,128,256]{3,2,1,0:T(8,128)(2,1)} %get-tuple-element.10.fetched, bf16[32,8,128,128]{3,2,1,0:T(8,128)(2,1)} %obs.3, ...), custom_call_target="tpu_custom_call" | custom-call | tf_op jit(solution)/shard_map/step_kernel/pallas_call | solution.py:558
  158.8 3.9 %last_step.1 = (f32[16,128,256]{2,1,0:T(8,128)}, f32[5,128,256]{2,1,0:T(8,128)}) custom-call(s32[8,8,128]{2,1,0:T(8,128)} %get-tuple-element.9.requested, bf16[32,128,256]{2,1,0:T(8,128)(2,1)} %bitcast.12, f32[16,128,256]{2,1,0:T(8,128)} %bitcast.9, f32[5,128,256]{2,1,0:T(8,128)} %get-tuple-element.13.store), custom_call_target="tpu_custom_call" | custom-call | tf_op jit(solution)/shard_map/last_step/pallas_call | solution.py:587

commit v5 on v3

--- a/solution.py
+++ b/solution.py
@@ -96,12 +96,13 @@
         s = order[i]
         later = jnp.minimum(i + 1, total - 1)
         xt = sku_buf[lax.rem(i, DEPTH)].T
+        gs = [jnp.dot(xt, misfits[k // 2], preferred_element_type=f32) for k in range(0, K, 2)]
+        for k in range(0, K, 2):
+            misfits[k // 2] = misfit(later, k)
         for k in range(0, K, 2):
             a, b = ids[k, s], ids[k + 1, s]
-            g = jnp.dot(xt, misfits[k // 2], preferred_element_type=f32)
-            misfits[k // 2] = misfit(later, k)
-            acc[a] += g[:, :BS]
-            acc[b] += g[:, BS:]
+            acc[a] += gs[k // 2][:, :BS]
+            acc[b] += gs[k // 2][:, BS:]
 
     n = VG // CHUNKS
     stores = []
@@ -152,10 +153,12 @@
             c.wait_send()
 
 
-def meet(peers):
+def meet(peers, meanwhile=None):
     barrier = pltpu.get_barrier_semaphore()
     for p in peers:
         pl.semaphore_signal(barrier, inc=1, device_id=p, device_id_type=MESH)
+    if meanwhile is not None:
+        meanwhile()
     pl.semaphore_wait(barrier, len(peers))
 
 
@@ -279,15 +282,18 @@
     ids_v[...] = jnp.zeros_like(ids_v)
     ids_v[0:1, 0:SLOTS] = ids[...]
     peers = [me.along_row(*p) for p in PLACES[:-1]]
-    meet(col_peers(me) + peers)
+
+    def cast():
+        load_store.wait()
+        low[...] = store_v[...].astype(bf16)
+
+    meet(col_peers(me) + peers, cast)
     wire = Wire(send_sem, recv_sem)
     asked = [
         wire.copy(ids_v, heard.at[me.row], me.along_row(*p)) for p in PLACES[:-1]
     ]
     own_ids = pltpu.make_async_copy(ids_v, heard.at[me.row], sems.at[2])
     own_ids.start()
-    load_store.wait()
-    low[...] = store_v[...].astype(bf16)
     gather = Gather(me, wire, low, group)
     keep_low = pltpu.make_async_copy(low, group.at[pl.ds(me.col * VB, VB)], sems.at[3])
     keep_low.start()

time: 152 us -> 152 us (level)
    pallas_call x1, Pallas kernels: 94.4 us -> 96 us  [local(): pl.pallas_call(step_kernel, out_shape=(jax.ShapeDtypeStruct((VB, BS, R),...]
    pallas_call x1, Pallas kernels: 15.3 us -> 13.7 us  [local(): pl.pallas_call(first_pass, out_shape=jax.ShapeDtypeStruct((VG, R, BS), bf...]
where the time goes in v5:
time: 152 us
  Pallas kernels  151 us (99%)
    pallas_call x1, Pallas kernels, local(): pl.pallas_call(step_kernel, out_shape=(jax.ShapeDtypeStruct((VB, BS, R),...  96 us
    pallas_call x1, Pallas kernels, local(): pl.pallas_call(gather_kernel, out_shape=(jax.ShapeDtypeStruct((VG, BS, R)...  37.6 us
    pallas_call x1, Pallas kernels, local(): pl.pallas_call(first_pass, out_shape=jax.ShapeDtypeStruct((VG, R, BS), bf...  13.7 us
    pallas_call x1, Pallas kernels, local(): pl.pallas_call(last_step, out_shape=(jax.ShapeDtypeStruct((UB, BS, R), f3...  3.87 us

profile of v5, /device:TPU:1, one launch (start us, length us, event | category | flops | bytes accessed | tf_op | source)
XLA Modules:
  0.0 151.8 jit_solution(14618159992922040082)
XLA Ops:
  0.6 37.6 %gather_kernel.1 = (bf16[80,128,256]{2,1,0:T(8,128)(2,1)}, bf16[8,4,128,256]{3,2,1,0:T(8,128)(2,1)}, s32[8,8,128]{2,1,0:T(8,128)}) custom-call(s32[1,32]{1,0:T(1,128)} %bitcast.17, f32[16,128,256]{2,1,0:T(8,128)} %bitcast.8, f32[5,128,256]{2,1,0:T(8,128)} %bitcast.10), custom_call_target="tpu_custom_call" | custom-call | tf_op jit(solution)/shard_map/gather_kernel/pallas_call | solution.py:496
  38.2 13.7 %first_pass.1.grad = bf16[80,256,128]{2,1,0:T(8,128)(2,1)} custom-call(s32[8,32]{1,0:T(8,128)} %bitcast.13, s32[8]{0:T(128)} %bitcast.15, bf16[8,4,128,256]{3,2,1,0:T(8,128)(2,1)} %get-tuple-element.10.fetched, bf16[32,8,128,128]{3,2,1,0:T(8,128)(2,1)} %obs.3, bf16[80,128,256]{2,1,0:T(8,128)(2,1)} %get-tuple-element.11.group), custom_call_target="tpu_custom_call" | custom-call | tf_op jit(solution)/shard_map/first_pass/pallas_call | solution.py:521
  51.9 96.0 %step_kernel.1 = (f32[5,128,256]{2,1,0:T(8,128)}, bf16[8,4,128,256]{3,2,1,0:T(8,128)(2,1)}) custom-call(s32[8,32]{1,0:T(8,128)} %bitcast.14, s32[8]{0:T(128)} %bitcast.16, bf16[80,256,128]{2,1,0:T(8,128)(2,1)} %first_pass.1.grad, bf16[8,4,128,256]{3,2,1,0:T(8,128)(2,1)} %get-tuple-element.10.fetched, bf16[32,8,128,128]{3,2,1,0:T(8,128)(2,1)} %obs.3, ...), custom_call_target="tpu_custom_call" | custom-call | tf_op jit(solution)/shard_map/step_kernel/pallas_call | solution.py:540
  147.9 3.9 %last_step.1 = (f32[16,128,256]{2,1,0:T(8,128)}, f32[5,128,256]{2,1,0:T(8,128)}) custom-call(s32[8,8,128]{2,1,0:T(8,128)} %get-tuple-element.9.requested, bf16[32,128,256]{2,1,0:T(8,128)(2,1)} %bitcast.12, f32[16,128,256]{2,1,0:T(8,128)} %bitcast.9, f32[5,128,256]{2,1,0:T(8,128)} %get-tuple-element.13.store), custom_call_target="tpu_custom_call" | custom-call | tf_op jit(solution)/shard_map/last_step/pallas_call | solution.py:569
